TPU v7x, 256 devices: a whole 4x4x8 slice. The times are simulated.
256 devices in a mesh: dp: 16 (over x_lo, y, core), mp: 8 (over z), side: 2 (over x_hi).
Axes of the slice: x: 4 (x_hi: 2, x_lo: 2; x = x_hi * 2 + x_lo), y: 4, z: 8, core: 2. Of those that a mesh axis runs over, the one named last changes fastest.
Arguments:
- tokens: bfloat16 [4096, 3072], P('dp', 'mp'), may hold values from -6 to 6
- up_weight: bfloat16 [2, 3072, 6144], P('side', 'dp', 'mp'), may hold values from -0.109375 to 0.109375
- down_weight: bfloat16 [2, 6144, 3072], P('side', 'mp', 'dp'), may hold values from -0.078125 to 0.078125
- mod_table: float32 [2, 50, 3, 3072], P('side'), may hold values from -3 to 3
- timesteps: int32 [16], P('dp'), may hold values from 0 to 49
- valid_counts: int32 [16], replicated, may hold values from 64 to 256, as said below
Outputs:
- block_out: bfloat16 [2, 4096, 3072], P('side', 'dp', 'mp')
- up_grads: float32 [3072, 6144], P(('dp', 'side'), 'mp')
- down_grads: float32 [6144, 3072], P('mp', ('dp', 'side'))
Inputs may be any that keep to these rules, and one draw needn't show every extreme that they name: `valid_counts`: every image has at least 64 valid tokens, and in every draw some image has all 256 valid.
All inputs are finite; a program needn't handle non-finite values.
Results may differ from a plain program's by a relative error of at most 0.018.
Values may be sent and summed in bfloat16 or wider, within the bound.
A program may use at most 64 MiB of HBM per device.

v0:
```python
import jax
import jax.numpy as jnp
from jax import lax
from jax.sharding import PartitionSpec as P


def passed_along(x, axis, by):
    peers = lax.axis_size(axis)
    pairs = [(i, i + by) for i in range(peers) if 0 <= i + by < peers]
    return lax.ppermute(x, axis, pairs)


def gelu_tanh(values):
    return jax.nn.gelu(values, approximate=True)


def shards(tokens, up_weight, down_weight, mod_table, timesteps, valid_counts):
    gathered = lax.all_gather(tokens, "mp", axis=1, tiled=True)
    width = gathered.shape[1]
    shard_width = tokens.shape[1]
    mp_offset = lax.axis_index("mp") * shard_width
    is_student = lax.axis_index("side") == 1
    wide = gathered.astype(jnp.float32)
    average = jnp.mean(wide, axis=-1, keepdims=True)
    centred = wide - average
    variance = jnp.mean(centred * centred, axis=-1, keepdims=True)
    scaled = centred * lax.rsqrt(variance + 1e-06)
    plan = mod_table.shape[1]
    one_hot = (jnp.arange(plan, dtype=jnp.int32)[None, :] == timesteps[0]).astype(jnp.float32)
    modulation = jnp.dot(
        one_hot,
        mod_table[0].reshape(plan, 3 * width),
        precision=lax.Precision.HIGHEST,
        preferred_element_type=jnp.float32,
    ).reshape(3, width)
    normed = (scaled * (1.0 + modulation[1]) + modulation[0]).astype(jnp.bfloat16)
    gate_row = modulation[2]
    hidden_pre = jnp.dot(
        normed,
        lax.all_gather(up_weight[0], "dp", axis=0, tiled=True),
        preferred_element_type=jnp.float32,
    )
    hidden_act = gelu_tanh(hidden_pre).astype(jnp.bfloat16)
    down_full = lax.all_gather(down_weight[0], "dp", axis=1, tiled=True)
    partial_value = jnp.dot(hidden_act, down_full, preferred_element_type=jnp.float32)
    positions = jnp.arange(normed.shape[0], dtype=jnp.int32)
    own_count = lax.dynamic_index_in_dim(valid_counts, lax.axis_index("dp"), 0, keepdims=False)
    valid_col = (positions < own_count).astype(jnp.float32)[:, None]
    valid_total = jnp.sum(valid_counts).astype(jnp.float32)
    mixed = lax.psum(partial_value.astype(jnp.bfloat16), "mp").astype(jnp.float32)
    out_full = (wide + gate_row * mixed).astype(jnp.bfloat16)
    out_local = lax.dynamic_slice_in_dim(out_full, mp_offset, shard_width, 1)
    other_full = passed_along(out_full, "side", 1)
    differ = out_full.astype(jnp.float32) - other_full.astype(jnp.float32)
    grad_out = (gate_row * differ * valid_col / jnp.sqrt(valid_total)).astype(jnp.bfloat16)

    def backprop():
        grad_act = lax.dot_general(
            grad_out, down_full, (((1,), (1,)), ((), ())), preferred_element_type=jnp.float32
        )
        unused, pullback = jax.vjp(gelu_tanh, hidden_pre)
        return pullback(grad_act)[0].astype(jnp.bfloat16)

    def no_backprop():
        return jnp.zeros(hidden_pre.shape, jnp.bfloat16)

    grad_pre = lax.cond(is_student, backprop, no_backprop)
    ff_width = hidden_act.shape[1]

    def product():
        return lax.dot_general(
            normed, grad_pre, (((0,), (0,)), ((), ())), preferred_element_type=jnp.float32
        )

    def nothing():
        return jnp.zeros(
            (width // lax.axis_size(("dp", "side")) * lax.axis_size(("dp", "side")), ff_width),
            jnp.float32,
        )

    up_share = lax.psum_scatter(
        lax.cond(is_student, product, nothing).astype(jnp.bfloat16),
        ("dp", "side"),
        scatter_dimension=0,
        tiled=True,
    ).astype(jnp.float32)

    def down_product():
        return lax.dot_general(
            hidden_act, grad_out, (((0,), (0,)), ((), ())), preferred_element_type=jnp.float32
        )

    def down_nothing():
        return jnp.zeros((ff_width, width), jnp.float32)

    down_term = lax.cond(is_student, down_product, down_nothing)
    down_share = lax.psum_scatter(
        down_term.astype(jnp.bfloat16), ("dp", "side"), scatter_dimension=1, tiled=True
    ).astype(jnp.float32)
    return (out_local[None], up_share, down_share)


def solution(mesh):
    placed = (
        P("dp", "mp"),
        P("side", "dp", "mp"),
        P("side", "mp", "dp"),
        P("side", None, None, None),
        P("dp"),
        P(),
    )
    return jax.shard_map(
        shards,
        mesh=mesh,
        in_specs=placed,
        out_specs=(P("side", "dp", "mp"), P(("dp", "side"), "mp"), P("mp", ("dp", "side"))),
        check_vma=False,
    )
```

profile of v0, /device:TPU:1, one launch (start us, length us, event | category | flops | bytes accessed | tf_op | source)
XLA Modules:
  0.0 593.4 jit_solution(2284106600337096998)
XLA Ops:
  7.2 0.0 all-gather.6.cloned.1.call-start
  7.2 0.7 all-gather.6.cloned.1.call-update
  7.9 0.0 all-gather.8.cloned.1.call-start
  7.9 0.7 all-gather.8.cloned.1.call-update
  8.6 0.0 all-gather.10.cloned.1.call-start
  8.7 0.7 all-gather.10.cloned.1.call-update
  9.4 0.0 all-reduce.2.cloned.1.call-start
  9.4 6.5 %reduce = f32[50,3,3072]{2,1,0:T(4,128)S(1)} reduce(f32[1,50,3,3072]{3,0,2,1:T(1,128)} %param.15, f32[]{:T(128)} %constant.65), dimensions={0}, to_apply=%param.15.reduce_sub_computation | reduce | bytes 3686404 | tf_op args[3]
  15.9 0.5 pad
  16.5 1.2 copy.14
  18.3 0.8 fusion.24
  19.1 29.2 %all-gather.6.cloned.1.call-done = bf16[256,3072]{1,0:T(8,128)(2,1)} async-done(((bf16[256,384]{1,0:T(8,128)(2,1)}), bf16[256,3072]{1,0:T(8,128)(2,1)}) %all-gather.6.cloned.1.call-update) | async-done | bytes 1572880 | tf_op jit(solution)/shard_map/all_gather | solution.py:18
  48.2 0.0 copy-start
  48.2 1.8 convert_reduce_fusion
  50.1 2.0 fusion.11
  52.0 0.0 copy-done
  52.0 0.8 fusion.14
  52.8 41.7 %all-gather.8.cloned.1.call-done = bf16[1,3072,768]{2,1,0:T(8,128)(2,1)} async-done(((bf16[1,192,768]{2,1,0:T(8,128)(2,1)}), bf16[1,3072,768]{2,1,0:T(8,128)(2,1)}) %all-gather.8.cloned.1.call-update) | async-done | bytes 4718608 | tf_op jit(solution)/shard_map/all_gather | solution.py:40
  94.5 4.6 fusion.23
  99.2 0.0 copy-start.1
  99.2 37.7 %all-gather.10.cloned.1.call-done = bf16[1,768,3072]{1,2,0:T(8,128)(2,1)} async-done(((bf16[1,768,192]{1,2,0:T(8,128)(2,1)}), bf16[1,768,3072]{1,2,0:T(8,128)(2,1)}) %all-gather.10.cloned.1.call-update) | async-done | bytes 4718608 | tf_op jit(solution)/shard_map/all_gather | solution.py:44
  136.9 4.9 convolution_convert_fusion
  141.8 0.0 copy-done.1
  141.8 0.0 copy-start.3
  141.8 0.0 all-reduce.2.cloned.1.call-update
  141.8 0.2 reduce-scatter.3.cloned.1.call-start
  142.1 74.3 %all-reduce.2.cloned.1.call-done = bf16[256,3072]{1,0:T(8,128)(2,1)} async-done(((bf16[256,3072]{1,0:T(8,128)(2,1)}), bf16[256,3072]{1,0:T(8,128)(2,1)}) %all-reduce.2.cloned.1.call-update) | async-done | bytes 1572880 | tf_op jit(solution)/shard_map/psum | solution.py:50
  216.3 3.1 fusion.15
  219.5 5.8 collective-permute-start
  225.2 0.0 copy-done.3
  225.2 0.6 reduce_sum.29
  226.6 0.6 dynamic_slice.8
  227.2 0.6 compare_convert_fusion
  227.8 25.6 %collective-permute-done = bf16[256,3072]{1,0:T(8,128)(2,1)} collective-permute-done((bf16[256,3072]{1,0:T(8,128)(2,1)}, bf16[256,3072]{1,0:T(8,128)(2,1)}, u32[]{:S(2)}, u32[]{:S(2)}) %collective-permute-start) | collective-permute-done | bytes 1572896 | tf_op jit(solution)/shard_map/ppermute | solution.py:10
  253.4 2.6 divide_convert_fusion
  256.0 0.1 conditional.3
  256.1 2.5 conditional.4
  256.1 2.5 broadcast.75
  258.6 0.0 copy-start.2
  258.6 0.0 reduce-scatter.3.cloned.1.call-update
  258.6 0.0 reduce-scatter.5.cloned.1.call-start
  258.6 0.9 copy-done.2
  259.6 2.8 conditional.5
  259.6 2.8 broadcast.76
  262.4 6.6 %copy.12 = bf16[768,3072]{0,1:T(8,128)(2,1)} copy(bf16[768,3072]{1,0:T(8,128)(2,1)} %get-tuple-element.43) | data formatting | bytes 9437184 | tf_op jit(solution)/shard_map/cond | solution.py:96
  269.0 0.0 reduce-scatter.5.cloned.1.call-update
  269.0 1.6 dynamic-slice_bitcast_fusion
  270.6 155.2 %reduce-scatter.3.cloned.1.call-done = bf16[96,768]{1,0:T(8,128)(2,1)} async-done(((bf16[3072,768]{1,0:T(8,128)(2,1)}), bf16[96,768]{1,0:T(8,128)(2,1)}) %reduce-scatter.3.cloned.1.call-update) | async-done | bytes 147472 | tf_op jit(solution)/shard_map/reduce_scatter | solution.py:81
  425.9 1.6 convert_element_type.71
  427.5 157.4 %reduce-scatter.5.cloned.1.call-done = bf16[768,96]{0,1:T(8,128)(2,1)} async-done(((bf16[768,3072]{0,1:T(8,128)(2,1)}), bf16[768,96]{0,1:T(8,128)(2,1)}) %reduce-scatter.5.cloned.1.call-update) | async-done | bytes 147472 | tf_op jit(solution)/shard_map/reduce_scatter | solution.py:97
  584.9 1.6 convert_element_type.73
  (4 shorter events, 0.1 us)
Async XLA Ops:
  7.2 41.1 %all-gather.6.cloned.1.call-start = ((), (), s32[]{:S(2)}) async-start(), calls=%async_computation.2 | async-start | bytes 1769472 | tf_op jit(solution)/shard_map/all_gather | solution.py:18
  7.9 86.6 %all-gather.8.cloned.1.call-start = ((), (), s32[]{:S(2)}) async-start(), calls=%async_computation.6 | async-start | bytes 5013504 | tf_op jit(solution)/shard_map/all_gather | solution.py:40
  8.6 128.2 %all-gather.10.cloned.1.call-start = ((), (), s32[]{:S(2)}) async-start(), calls=%async_computation.7 | async-start | bytes 5013504 | tf_op jit(solution)/shard_map/all_gather | solution.py:44
  9.4 207.0 %all-reduce.2.cloned.1.call-start = ((), (), s32[]{:S(2)}) async-start(), calls=%async_computation.3 | async-start | bytes 3145728 | tf_op jit(solution)/shard_map/psum | solution.py:50
  48.2 3.8 copy-start
  99.2 42.7 %copy-start.1 = (bf16[256,768]{1,0:T(8,128)(2,1)}, bf16[256,768]{1,0:T(8,128)(2,1)S(1)}, u32[]{:S(2)}) copy-start(bf16[256,768]{1,0:T(8,128)(2,1)S(1)} %get-tuple-element.39) | copy-start | bytes 1179652
  141.8 83.4 %copy-start.3 = (s32[16]{0:T(128)S(1)}, s32[16]{0:T(128)}, u32[]{:S(2)}) copy-start(s32[16]{0:T(128)} %param.17) | copy-start | bytes 196
  141.8 284.0 %reduce-scatter.3.cloned.1.call-start = ((), (), s32[]{:S(2)}) async-start(), calls=%async_computation.4 | async-start | bytes 4866048 | tf_op jit(solution)/shard_map/reduce_scatter | solution.py:81
  219.5 34.0 %collective-permute-start = (bf16[256,3072]{1,0:T(8,128)(2,1)}, bf16[256,3072]{1,0:T(8,128)(2,1)}, u32[]{:S(2)}, u32[]{:S(2)}) collective-permute-start(bf16[256,3072]{1,0:T(8,128)(2,1)} %fusion.15), channel_id=1, source_target_pairs={{0,1},{2,3},{4,5},{6,7},{8,9},{10,11},{12,13},{14,15},{16,17},{18,... | collective-permute-start | bytes 4718600 | tf_op jit(solution)/shard_map/ppermute | solution.py:10
  258.6 1.0 copy-start.2
  258.6 326.3 %reduce-scatter.5.cloned.1.call-start = ((), (), s32[]{:S(2)}) async-start(), calls=%async_computation.5 | async-start | bytes 4866048 | tf_op jit(solution)/shard_map/reduce_scatter | solution.py:97
Sparse Core Ops, SparseCore 0:
  9.8 38.4 all-gather.5
  50.1 44.3 all-gather.7
  96.4 40.4 all-gather.9
  142.0 74.3 all-reduce.1
  258.7 167.0 reduce-scatter.2
  428.2 156.6 reduce-scatter.4
where the time goes:
time: 594 us; the launch traced here: 593 us
  waiting for transfers between devices  523 us (88%)
  other arithmetic  21.3 us (4%)
  local copies, waits for them, and re-layouts  16.8 us (3%)
  between operations  15.5 us (3%)
  matrix products  10.3 us (2%)
  starting transfers between devices  6.19 us (1%)
    reduce_scatter x1, waiting for transfers between devices, shards(): lax.psum_scatter(down_term.astype(jnp.bfloat16), ('dp', 'side'), scatter_...  157 us
    reduce_scatter x1, waiting for transfers between devices, shards(): lax.psum_scatter(lax.cond(is_student, product, nothing).astype(jnp.bfloat...  155 us
    psum x1, waiting for transfers between devices, shards(): lax.psum(partial_value.astype(jnp.bfloat16), 'mp').astype(jnp.float32)  74.3 us
    all_gather x1, waiting for transfers between devices, shards(): lax.all_gather(up_weight[0], 'dp', axis=0, tiled=True)  41.7 us
    all_gather x1, waiting for transfers between devices, shards(): down_full = lax.all_gather(down_weight[0], 'dp', axis=1, tiled=True)  37.7 us
    all_gather x1, waiting for transfers between devices, shards(): gathered = lax.all_gather(tokens, 'mp', axis=1, tiled=True)  29.2 us
    ppermute x1, waiting for transfers between devices, passed_along(): return lax.ppermute(x, axis, pairs)  25.6 us
  transfers between devices with their start and end apart: 7, of which 7 were waited for; matrix products, arithmetic and copies ran while one was open for 6% of the time, Pallas kernels for 0%

commit v1 on v0

v1 whole, which is shorter than its diff:
```python
import functools

import jax
import jax.numpy as jnp
from jax import lax
from jax.experimental import pallas as pl
from jax.experimental.pallas import tpu as pltpu
from jax.sharding import PartitionSpec as P

BF = jnp.bfloat16
F32 = jnp.float32
R = 4
ROWS = 192 // R
RA = 32
NZ = 8
SEQ = 256
BLK = 384
N_SEM = 300


def gelu_pair(v):
    k = 0.7978845608028654
    v2 = v * v
    t = jnp.tanh(k * v * (1.0 + 0.044715 * v2))
    half = 0.5 * (1.0 + t)
    act = v * half
    slope = half + 0.5 * v * (1.0 - t * t) * (k * (1.0 + 3.0 * 0.044715 * v2))
    return act, slope


def nn(a, b):
    return lax.dot_general(a, b, (((1,), (0,)), ((), ())), preferred_element_type=F32)


def nt(a, b):
    return lax.dot_general(a, b, (((1,), (1,)), ((), ())), preferred_element_type=F32)


def tn(a, b):
    return lax.dot_general(a, b, (((0,), (0,)), ((), ())), preferred_element_type=F32)


def kernel(
    axes,
    tok_ref, up_ref, downt_ref, mod_ref, gate_ref, valid_ref,
    out_ref, ug_ref, dg_ref,
    T, U, D, N, NTR, HP, SL, ACT, PO, PS, PR, ZS, ZR, GATE, TOKT, OTA, OTB, GT, GA, GP,
    QV, XBS, XBR, A2S, A2R, A1S, A1R, B2S, B2R, B1S, B1R, AXS, AXR, FS, FO, FR, HS, HR,
    send, recv, local,
):
    dp, z, s = lax.axis_index("dp"), lax.axis_index("mp"), lax.axis_index("side")
    c = lax.rem(dp, 2)
    y = lax.rem(lax.div(dp, 2), 4)
    xl = lax.div(dp, 8)
    xo = 1 - xl
    yp, ym, y2 = lax.rem(y + 1, 4), lax.rem(y + 3, 4), lax.rem(y + 2, 4)
    oc = 1 - c

    def zz(k):
        return lax.rem(z + (k + NZ), NZ)

    def where(dp_=None, mp_=None, side_=None):
        at = {"dp": dp if dp_ is None else dp_, "mp": z if mp_ is None else mp_, "side": s if side_ is None else side_}
        return tuple(at[a] for a in axes)

    def jj(a, b):
        return a * 4 + b

    X = where(dp_=xo * 8 + y * 2 + c)
    YP = where(dp_=xl * 8 + yp * 2 + c)
    YM = where(dp_=xl * 8 + ym * 2 + c)
    ZP = where(mp_=zz(1))
    ZM = where(mp_=zz(-1))
    C = where(dp_=dp + 1 - 2 * c)
    S = where(side_=1 - s)

    barrier = pltpu.get_barrier_semaphore()
    peers = (X, YP, YM, ZP, ZM, C, S)
    for peer in peers:
        pl.semaphore_signal(barrier, inc=1, device_id=peer, device_id_type=pl.DeviceIdType.MESH)
    pl.semaphore_wait(barrier, len(peers))

    used = [0]
    started = {None: [], 0: [], 1: []}

    class Copy:
        def __init__(self, refs, dev, side):
            self.refs, self.dev, self.i = refs, dev, used[0]
            used[0] += 1
            self.made().start()
            started[side].append(self)

        def made(self):
            src, dst = self.refs()
            return pltpu.make_async_remote_copy(
                src_ref=src, dst_ref=dst, send_sem=send.at[self.i], recv_sem=recv.at[self.i],
                device_id=self.dev, device_id_type=pl.DeviceIdType.MESH,
            )

        def wait_recv(self):
            self.made().wait_recv()

        def wait_send(self):
            self.made().wait_send()

    def copy(src, dst, dev, side=None):
        return Copy(lambda: (src(), dst()), dev, side)

    def copy_same(at, dev, side=None):
        return Copy(lambda: (at(),) * 2, dev, side)

    student = s == 1

    class Gather:
        def __init__(self, buf, ra):
            self.buf, self.ra = buf, ra

        def g0(self):
            self.xa = copy_same(lambda: self.apart(xl, y), X)
            self.yp = copy_same(lambda: self.buf(own), YP)
            self.ym = copy_same(lambda: self.buf(own), YM)
            self.xb = copy_same(lambda: self.bpart(xl, y), X)

        def g1(self):
            self.xa.wait_recv()
            self.xap = copy_same(lambda: self.apart(xo, y), YP)
            self.xam = copy_same(lambda: self.apart(xo, y), YM)

        def apart(self, xx, yy):
            return self.buf(jj(xx, yy)).at[:, pl.ds(0, self.ra)]

        def bpart(self, xx, yy):
            b = self.buf(jj(xx, yy))
            return b.at[:, pl.ds(self.ra, b.shape[1] - self.ra)]

        def g2(self):
            self.yp.wait_recv()
            self.rp = copy_same(lambda: self.buf(jj(xl, ym)).at[0], YP)
            self.bxm = copy_same(lambda: self.bpart(xl, ym), X)
            self.ym.wait_recv()
            self.rm = copy_same(lambda: self.buf(jj(xl, yp)).at[1], YM)
            self.bxp = copy_same(lambda: self.bpart(xl, yp), X)

        def g3(self):
            self.xap.wait_recv()
            self.rxp = copy_same(lambda: self.buf(jj(xo, ym)).at[0, pl.ds(0, self.ra)], YP)
            self.xam.wait_recv()
            self.rxm = copy_same(lambda: self.buf(jj(xo, yp)).at[1, pl.ds(0, self.ra)], YM)

        def g4(self):
            self.rp.wait_recv()
            self.rm.wait_recv()
            self.bx2 = copy_same(lambda: self.bpart(xl, y2), X)

        def g5(self):
            for d in (self.xb, self.bxm, self.bxp, self.rxp, self.rxm, self.bx2):
                d.wait_recv()

    own = jj(xl, y)
    u_out = copy(lambda: up_ref.at[:, pl.ds(pl.multiple_of(oc * BLK, 128), BLK)], lambda: U.at[own, c], C)
    d_out = copy(lambda: downt_ref.at[oc], lambda: D.at[:, own, c], C)
    tok_in = pltpu.make_async_copy(tok_ref, T.at[z], local.at[0])
    tok_in.start()
    u_in = pltpu.make_async_copy(up_ref.at[:, pl.ds(pl.multiple_of(c * BLK, 128), BLK)], U.at[own, c], local.at[1])
    u_in.start()
    d_in = pltpu.make_async_copy(downt_ref.at[c], D.at[:, own, c], local.at[2])
    d_in.start()

    tk = {}

    def tok_send(hop):
        for p in range(2):
            rows = pl.ds(128 * p, 128)
            if hop:
                if ("+", hop - 1, p) in tk:
                    tk["+", hop - 1, p].wait_recv()
            at = functools.partial(lambda k, rows: tok_ref.at[rows] if k is None else T.at[zz(k), rows], rows=rows)
            src = functools.partial(at, None if hop == 0 else -hop)
            if hop < 3 or p == 0:
                tk["+", hop, p] = copy(src, functools.partial(at, -hop), ZP)
            if hop:
                if ("-", hop - 1, p) in tk:
                    tk["-", hop - 1, p].wait_recv()
            src = functools.partial(at, None if hop == 0 else hop)
            if hop < 3 or p == 1:
                tk["-", hop, p] = copy(src, functools.partial(at, hop), ZM)

    gu = Gather(lambda j: U.at[j], 128)
    gd = [Gather(functools.partial(lambda r, j: D.at[r, j], r), RA) for r in range(R)]

    tok_send(0)
    u_in.wait()
    u_out.wait_recv()
    gu.g0()
    tok_in.wait()
    gate = jnp.transpose(jnp.broadcast_to(gate_ref[0:1, :], (128, BLK)))
    GATE[:, 0:128] = gate
    GATE[:, 128:256] = gate
    tt = jnp.transpose(T[z].astype(F32))
    TOKT[...] = tt
    tok_send(1)
    gu.g1()
    tok_send(2)
    gu.g2()
    gu.g3()
    tok_send(3)
    gu.g4()
    d_in.wait()
    d_out.wait_recv()
    gd[0].g0()
    tk["+", 3, 0].wait_recv()
    tk["-", 3, 1].wait_recv()

    def norm_rows(i, carry):
        rows = pl.ds(pl.multiple_of(i * 16, 16), 16)
        x = [T[b, rows].astype(F32) for b in range(NZ)]
        total = x[0]
        for b in range(1, NZ):
            total = total + x[b]
        mean = jnp.sum(total, axis=-1, keepdims=True) * (1.0 / (NZ * BLK))
        x = [v - mean for v in x]
        sq = x[0] * x[0]
        for b in range(1, NZ):
            sq = sq + x[b] * x[b]
        var = jnp.sum(sq, axis=-1, keepdims=True) * (1.0 / (NZ * BLK))
        rs = lax.rsqrt(var + 1e-06)
        for b in range(NZ):
            cols = slice(b * BLK, (b + 1) * BLK)
            n = x[b] * rs * (1.0 + mod_ref[1:2, cols]) + mod_ref[0:1, cols]
            N[c, b, rows] = n.astype(BF)
        return carry

    n_out = []
    for p in range(2):
        lax.fori_loop(8 * p, 8 * p + 8, norm_rows, 0)
        rows = pl.ds(128 * p, 128)
        n_out.append(copy_same(functools.partial(lambda rows: N.at[c, :, rows], rows), C))

    gu.g5()

    def hidden(img):
        h = nn(N[img, 0], U[0].reshape(BLK, BLK))
        for b in range(1, NZ):
            h = h + nn(N[img, b], U[b].reshape(BLK, BLK))
        HP[...] = h

        def act_rows(i, carry):
            rows = pl.ds(pl.multiple_of(i * 32, 32), 32)
            a, g = gelu_pair(HP[rows])
            ACT[img, rows] = a.astype(BF)
            SL[img, rows] = g
            return carry

        lax.fori_loop(0, SEQ // 32, act_rows, 0)

    def hidden_loop(i, carry):
        @pl.when(i == 1)
        def _():
            for d in n_out:
                d.wait_recv()

        hidden(lax.rem(c + i, 2))
        return carry

    gd[0].g1()
    lax.fori_loop(0, 2, hidden_loop, 0)

    m_out, zs = {}, {}

    def mixed(r):
        w = D[r].reshape(NZ * 2 * ROWS, BLK)
        PS[r] = nt(w, ACT[oc]).astype(BF)
        m_out[r] = copy(lambda: PS.at[r], lambda: PR.at[r], C)
        PO[r] = nt(w, ACT[c])

    def val(r, b):
        rows = pl.ds(pl.multiple_of(b * 2 * ROWS, 32), 2 * ROWS)
        return PO[r, rows] + PR[r, rows].astype(F32)

    def zstage(r, k):
        h0, h1 = pl.ds(0, ROWS), pl.ds(ROWS, ROWS)
        if k == 0:
            m_out[r].wait_recv()
            v = val(r, zz(4)).astype(BF)
            ZS[r, 0, 0] = v
            zs[r, 0, 0] = copy(lambda: ZS.at[r, 0, 0, h0], lambda: ZR.at[r, 0, 0, h0], ZP)
            zs[r, 1, 0] = copy(lambda: ZS.at[r, 0, 0, h1], lambda: ZR.at[r, 1, 0, h1], ZM)
            return
        for q in range(2):
            zs[r, q, k - 1].wait_recv()
            v = val(r, zz((4 - k) if q == 0 else (k - 4)))
            if k == 1:
                h = slice(0, ROWS) if q == 0 else slice(ROWS, 2 * ROWS)
                g = slice(ROWS, 2 * ROWS) if q == 0 else slice(0, ROWS)
                ZS[r, q, k, h] = (v[h] + ZR[r, q, 0, h].astype(F32)).astype(BF)
                ZS[r, q, k, g] = v[g].astype(BF)
            else:
                ZS[r, q, k] = (v + ZR[r, q, k - 1].astype(F32)).astype(BF)
            at = functools.partial(lambda ref, q: ref.at[r, q, k], q=q)
            zs[r, q, k] = copy(functools.partial(at, ZS), functools.partial(at, ZR), ZP if q == 0 else ZM)

    sw = {}

    def rows_of(r, h):
        return slice(192 * h + ROWS * r, 192 * h + ROWS * (r + 1))

    def output(r):
        zs[r, 0, 3].wait_recv()
        zs[r, 1, 3].wait_recv()
        m = val(r, z) + ZR[r, 0, 3].astype(F32) + ZR[r, 1, 3].astype(F32)
        for h in range(2):
            w = rows_of(r, h)
            o = (TOKT[w] + GATE[w] * m[ROWS * h:ROWS * (h + 1)]).astype(BF)
            OTA[r, h] = o
            TOKT[w] = o.astype(F32)

        @pl.when(s == 0)
        def _():
            sw[r] = copy(lambda: OTA.at[r], lambda: OTB.at[r], S, 0)

    ag, fw = {}, {}

    def gslice(r, img, b, h):
        n = ROWS if h is not None else 2 * ROWS
        return GT.at[r, img, pl.ds(pl.multiple_of(b * 2 * ROWS + (h or 0) * ROWS, 16), n)]

    def astage(r, k):
        @pl.when(student)
        def _():
            def push(kk, dev, h=None):
                return copy_same(lambda: gslice(r, c, zz(kk), h), dev, 1)

            if k == 0:
                sw[r].wait_recv()
                vrow = valid_ref[0:1, :]
                for h in range(2):
                    w = rows_of(r, h)
                    diff = OTA[r, h].astype(F32) - OTB[r, h].astype(F32)
                    rows = pl.ds(pl.multiple_of(z * 2 * ROWS + h * ROWS, 16), ROWS)
                    GT[r, c, rows] = (GATE[w] * diff * vrow).astype(BF)
                ag[r, 0, 0] = push(0, ZP)
                ag[r, 1, 0] = push(0, ZM)
                fw[r, 0] = [push(0, C)]
                return
            ag[r, 0, k - 1].wait_recv()
            h = 0 if k > 2 else None
            if k < 4:
                ag[r, 0, k] = push(-k, ZP, h)
            fw[r, k] = [push(-k, C, None if k < 4 else 0)]
            ag[r, 1, k - 1].wait_recv()
            h = 1 if k > 2 else None
            if k < 4:
                ag[r, 1, k] = push(k, ZM, h)
            fw[r, k].append(push(k, C, None if k < 4 else 1))

    class Reduce:
        def __init__(self, kind, r):
            self.i = kind * R + r
            self.r, self.kind = r, kind

        def both(self, src, dst):
            def one(h):
                return copy(lambda: src.at[self.i, h], lambda: dst.at[self.i, h], (YP, YM)[h], 1)

            return [one(0), one(1)]

        def q(self, j, rows):
            return QV[self.kind, j, :, rows]

        def r0(self):
            i, a, b = self.i, slice(0, RA), slice(RA, ROWS)
            for h in range(2):
                for x in range(2):
                    A2S[i, h, x] = QV[self.kind, jj(x, y2), h, a].astype(BF)
            self.a2 = self.both(A2S, A2R)
            for k in range(4):
                XBS[i, k] = QV[self.kind, jj(xo, k), :, b].astype(BF)
            self.xb = copy(lambda: XBS.at[i], lambda: XBR.at[i], X, 1)

        def r1(self):
            i, a = self.i, slice(0, RA)
            for h in range(2):
                self.a2[h].wait_recv()
                for x in range(2):
                    v = self.q(jj(x, (yp, ym)[h]), a)
                    A1S[i, h, x, h] = (v[h] + A2R[i, h, x].astype(F32)).astype(BF)
                    A1S[i, h, x, 1 - h] = v[1 - h].astype(BF)
            self.a1 = self.both(A1S, A1R)

        def r2(self):
            i, b = self.i, slice(RA, ROWS)
            self.xb.wait_recv()
            v = self.q(jj(xl, y2), b) + XBR[i, y2].astype(F32)
            B2S[i] = v.astype(BF)
            self.b2 = self.both(B2S, B2R)

        def r3(self):
            i, b = self.i, slice(RA, ROWS)
            for h in range(2):
                self.b2[h].wait_recv()
                yy = (yp, ym)[h]
                v = self.q(jj(xl, yy), b) + XBR[i, yy].astype(F32)
                B1S[i, h, h] = (v[h] + B2R[i, h].astype(F32)).astype(BF)
                B1S[i, h, 1 - h] = v[1 - h].astype(BF)
            self.b1 = self.both(B1S, B1R)

        def r4(self):
            i, a = self.i, slice(0, RA)
            for h in range(2):
                self.a1[h].wait_recv()
            v = self.q(jj(xo, y), a) + A1R[i, 0, xo].astype(F32) + A1R[i, 1, xo].astype(F32)
            AXS[i] = v.astype(BF)
            self.ax = copy(lambda: AXS.at[i], lambda: AXR.at[i], X, 1)

        def r5(self):
            i, a, b = self.i, slice(0, RA), slice(RA, ROWS)
            for d in (self.ax, *self.b1):
                d.wait_recv()
            va = self.q(own, a) + A1R[i, 0, xl].astype(F32) + A1R[i, 1, xl].astype(F32) + AXR[i].astype(F32)
            vb = self.q(own, b) + XBR[i, y].astype(F32) + B1R[i, 0].astype(F32) + B1R[i, 1].astype(F32)
            FO[i, :, a] = va
            FO[i, :, b] = vb
            FS[i] = FO[i, oc].astype(BF)
            self.f = copy(lambda: FS.at[i], lambda: FR.at[i], C, 1)

        def r6(self):
            i = self.i
            self.f.wait_recv()
            if self.r < R // 2:
                HS[i, c] = FO[i, c].astype(BF)
                HS[i, oc] = FR[i]
                self.h = copy(lambda: HS.at[i], lambda: HR.at[i], S, 1)
            else:
                o = (ug_ref, dg_ref)[self.kind]
                rows = slice(ROWS * (self.r - R // 2), ROWS * (self.r - R // 2 + 1))

                @pl.when(c == 0)
                def _():
                    o[rows, 0:BLK] = FO[i, 0]
                    o[rows, BLK:2 * BLK] = FR[i].astype(F32)

                @pl.when(c == 1)
                def _():
                    o[rows, 0:BLK] = FR[i].astype(F32)
                    o[rows, BLK:2 * BLK] = FO[i, 1]

    red = {(k, r): Reduce(k, r) for k in range(2) for r in range(R)}

    def down_grads(r):
        g = [GT[r, 0], GT[r, 1]]
        q = nn(g[0], ACT[0]) + nn(g[1], ACT[1])
        QV[1] = q.reshape(NZ, 2, ROWS, BLK)

    def grad_act(r):
        w = D[r].reshape(NZ * 2 * ROWS, BLK)
        for img in range(2):
            v = tn(GT[r, img], w)
            if r == 0:
                GA[img] = v
            else:
                GA[img] += v

    def arrived(r):
        for k in range(5):
            for d in fw[r, k]:
                d.wait_recv()

    def transposed():
        @pl.when(student)
        def _():
            def one(i, carry):
                img, j = lax.div(i, 8), lax.rem(i, 8)
                t = jnp.transpose(N[img, j].astype(F32)).astype(BF)
                for r in range(R):
                    for h in range(2):
                        NTR[r, img, pl.ds(pl.multiple_of(j * 2 * ROWS + h * ROWS, 16), ROWS)] = t[rows_of(r, h)]
                return carry

            lax.fori_loop(0, 16, one, 0)

    for r in range(R):
        if r:
            gd[r].g1()
        if r > 1:
            zstage(r - 2, 3)
        if r + 1 < R:
            gd[r + 1].g0()
        if r > 0:
            zstage(r - 1, 1)
        if r == 1:
            transposed()
        gd[r].g2()
        if r > 2:
            output(r - 3)
        gd[r].g3()
        if r > 0:
            zstage(r - 1, 2)
        if r > 2:
            astage(r - 3, 0)
        gd[r].g4()
        gd[r].g5()
        mixed(r)
        zstage(r, 0)
    zstage(R - 2, 3)
    zstage(R - 1, 1)
    output(R - 3)
    zstage(R - 1, 2)
    output(R - 2)
    astage(R - 3, 0)
    zstage(R - 1, 3)
    astage(0, 1)
    output(R - 1)
    astage(R - 2, 0)
    astage(1, 1)
    astage(0, 2)
    astage(R - 1, 0)
    astage(2, 1)
    astage(1, 2)
    astage(0, 3)
    astage(3, 1)
    astage(2, 2)
    astage(1, 3)
    astage(0, 4)
    astage(3, 2)
    astage(2, 3)

    out_ref[...] = jnp.transpose(TOKT[...]).astype(BF)

    @pl.when(student)
    def _():
        arrived(0)
        down_grads(0)
        red[1, 0].r0()

    astage(1, 4)
    astage(3, 3)
    astage(2, 4)

    @pl.when(student)
    def _():
        grad_act(0)
        red[1, 0].r1()
        red[1, 0].r2()

    astage(3, 4)

    @pl.when(student)
    def _():
        red[1, 0].r3()
        red[1, 0].r4()
        order = [(1, r) for r in range(R)] + [(0, r) for r in range(R)]

        def first(k, r):
            if k == 1:
                arrived(r)
                down_grads(r)
            else:
                if r == 0:
                    for img in range(2):
                        GP[img] = (GA[img] * SL[img]).astype(BF)
                q = nn(NTR[r, 0], GP[0]) + nn(NTR[r, 1], GP[1])
                QV[0] = q.reshape(NZ, 2, ROWS, BLK)
            red[k, r].r0()

        for n in range(1, 2 * R):
            k, r = order[n]
            prev = red[order[n - 1]]
            if n > 1:
                prev.r3()
                prev.r4()
            prev.r5()
            first(k, r)
            if k == 1:
                grad_act(r)
            prev.r6()
            red[k, r].r1()
            red[k, r].r2()
        last = red[order[-1]]
        last.r3()
        last.r4()
        last.r5()
        last.r6()

    @pl.when(s == 0)
    def _():
        for k in (1, 0):
            o = (ug_ref, dg_ref)[k]
            for r in range(R // 2):
                red[k, r].h.wait_recv()
                for h in range(2):
                    o[ROWS * r:ROWS * (r + 1), BLK * h:BLK * (h + 1)] = HR[k * R + r, h].astype(F32)

    for d in started[None]:
        d.wait_send()

    @pl.when(s == 0)
    def _():
        for d in started[0]:
            d.wait_send()

    @pl.when(student)
    def _():
        for d in started[1]:
            d.wait_send()


def shards(axes, tokens, up_weight, down_weight, mod_table, timesteps, valid_counts):
    mp, dp = lax.axis_index("mp"), lax.axis_index("dp")
    mod = lax.dynamic_index_in_dim(mod_table[0], timesteps[0], 0, keepdims=False)
    gate = jnp.broadcast_to(lax.dynamic_slice_in_dim(mod[2], mp * BLK, BLK)[None], (8, BLK))
    count = lax.dynamic_index_in_dim(valid_counts, dp, 0, keepdims=False)
    total = jnp.sum(valid_counts).astype(F32)
    valid = (jnp.arange(SEQ, dtype=jnp.int32) < count).astype(F32) / jnp.sqrt(total)
    valid = jnp.broadcast_to(valid[None], (8, SEQ))
    downt = down_weight[0].reshape(2, BLK, R, ROWS).transpose(0, 2, 3, 1)

    v = pltpu.VMEM
    nred = 2 * R
    scratch = [
        v((NZ, SEQ, BLK), BF),
        v((NZ, 2, 192, BLK), BF),
        v((R, NZ, 2, ROWS, BLK), BF),
        v((2, NZ, SEQ, BLK), BF),
        v((R, 2, NZ * 2 * ROWS, SEQ), BF),
        v((SEQ, BLK), F32),
        v((2, SEQ, BLK), F32),
        v((2, SEQ, BLK), BF),
        v((R, NZ * 2 * ROWS, SEQ), F32),
        v((R, NZ * 2 * ROWS, SEQ), BF),
        v((R, NZ * 2 * ROWS, SEQ), BF),
        v((R, 2, 4, 2 * ROWS, SEQ), BF),
        v((R, 2, 4, 2 * ROWS, SEQ), BF),
        v((BLK, SEQ), F32),
        v((BLK, SEQ), F32),
        v((R, 2, ROWS, SEQ), BF),
        v((R, 2, ROWS, SEQ), BF),
        v((R, 2, NZ * 2 * ROWS, SEQ), BF),
        v((2, SEQ, BLK), F32),
        v((2, SEQ, BLK), BF),
        v((2, NZ, 2, ROWS, BLK), F32),
        v((nred, 4, 2, ROWS - RA, BLK), BF),
        v((nred, 4, 2, ROWS - RA, BLK), BF),
        v((nred, 2, 2, RA, BLK), BF),
        v((nred, 2, 2, RA, BLK), BF),
        v((nred, 2, 2, 2, RA, BLK), BF),
        v((nred, 2, 2, 2, RA, BLK), BF),
        v((nred, 2, ROWS - RA, BLK), BF),
        v((nred, 2, ROWS - RA, BLK), BF),
        v((nred, 2, 2, ROWS - RA, BLK), BF),
        v((nred, 2, 2, ROWS - RA, BLK), BF),
        v((nred, 2, RA, BLK), BF),
        v((nred, 2, RA, BLK), BF),
        v((nred, ROWS, BLK), BF),
        v((nred, 2, ROWS, BLK), F32),
        v((nred, ROWS, BLK), BF),
        v((nred, 2, ROWS, BLK), BF),
        v((nred, 2, ROWS, BLK), BF),
        pltpu.SemaphoreType.DMA((N_SEM,)),
        pltpu.SemaphoreType.DMA((N_SEM,)),
        pltpu.SemaphoreType.DMA((3,)),
    ]
    hbm = pl.BlockSpec(memory_space=pl.ANY)
    vm = pl.BlockSpec(memory_space=pltpu.VMEM)
    out, up, down = pl.pallas_call(
        functools.partial(kernel, axes),
        out_shape=(
            jax.ShapeDtypeStruct((SEQ, BLK), BF),
            jax.ShapeDtypeStruct((96, 2 * BLK), F32),
            jax.ShapeDtypeStruct((96, 2 * BLK), F32),
        ),
        in_specs=[hbm, hbm, hbm, vm, vm, vm],
        out_specs=(vm, vm, vm),
        scratch_shapes=scratch,
        compiler_params=pltpu.CompilerParams(
            collective_id=0, has_side_effects=True, vmem_limit_bytes=67043328
        ),
    )(tokens, up_weight[0], downt, mod, gate, valid)
    return out[None], up, down.T


def solution(mesh):
    placed = (
        P("dp", "mp"),
        P("side", "dp", "mp"),
        P("side", "mp", "dp"),
        P("side", None, None, None),
        P("dp"),
        P(),
    )
    return jax.shard_map(
        functools.partial(shards, mesh.axis_names),
        mesh=mesh,
        in_specs=placed,
        out_specs=(P("side", "dp", "mp"), P(("dp", "side"), "mp"), P("mp", ("dp", "side"))),
        check_vma=False,
    )
```

time: 594 us -> 232 us (0.39)
  the two profiles are of different devices: /device:TPU:1 before, /device:TPU:5 now
where the time goes in v1:
time: 232 us; the launch traced here: 231 us
  Pallas kernels  216 us (93%)
  local copies, waits for them, and re-layouts  11.3 us (5%)
    pallas_call x1, Pallas kernels, shards(): pl.pallas_call(functools.partial(kernel, axes), out_shape=(jax.ShapeDtype...  216 us
    unnamed x4, local copies, waits for them, and re-layouts  5.64 us

profile of v1, /device:TPU:5, one launch (start us, length us, event | category | flops | bytes accessed | tf_op | source)
XLA Modules:
  0.0 231.4 jit_solution(9241480054009850075)
XLA Ops:
  1.3 1.3 reduce_sum.9
  3.3 1.2 dynamic_slice.13
  4.5 0.6 compare_select_fusion
  5.2 0.7 dynamic-slice_reduce_fusion
  5.9 0.6 broadcast_in_dim.19.valid_ref
  6.5 0.6 broadcast_in_dim.18.gate_ref
  7.1 0.8 constant_dynamic-slice_fusion
  7.8 0.6 copy.14
  8.5 1.0 reshape_squeeze.3
  9.5 0.7 copy.13
  10.3 216.1 %shard_map.85 = (bf16[256,384]{1,0:T(8,128)(2,1)}, f32[96,768]{1,0:T(8,128)}, f32[96,768]{1,0:T(8,128)}) custom-call(bf16[256,384]{1,0:T(8,128)(2,1)} %tok_ref.1, bf16[192,768]{1,0:T(8,128)(2,1)} %bitcast.17, bf16[2,4,48,384]{3,2,1,0:T(8,128)(2,1)} %bitcast.16, f32[3,3072]{1,0:T(4,128)} %bitcast.20, f32[8,384]{1,0:T(8,128)} %broadcast_in_dim.18.gate_ref, ...), custom_call_target="tpu_custom_call" | custom-call | tf_op jit(solution)/shard_map/pallas_call | solution.py:664
  226.3 1.6 copy.19
  228.0 1.7 copy.20
  229.7 1.7 copy.21

commit v2 on v1

--- a/solution.py
+++ b/solution.py
@@ -15,7 +15,8 @@
 NZ = 8
 SEQ = 256
 BLK = 384
-N_SEM = 300
+N_RECV = 290
+N_SEND = {None: 32, 0: 4, 1: 32}
 
 
 def gelu_pair(v):
@@ -42,7 +43,7 @@
 
 def kernel(
     axes,
-    tok_ref, up_ref, downt_ref, mod_ref, gate_ref, valid_ref,
+    tok_ref, up_ref, downt_ref, mod_ref, counts_ref,
     out_ref, ug_ref, dg_ref,
     T, U, D, N, NTR, HP, SL, ACT, PO, PS, PR, ZS, ZR, GATE, TOKT, OTA, OTB, GT, GA, GP,
     QV, XBS, XBR, A2S, A2R, A1S, A1R, B2S, B2R, B1S, B1R, AXS, AXR, FS, FO, FR, HS, HR,
@@ -87,13 +88,18 @@
         def __init__(self, refs, dev, side):
             self.refs, self.dev, self.i = refs, dev, used[0]
             used[0] += 1
+            mine = started[side]
+            pool = N_SEND[side]
+            self.j = len(mine) % pool + {None: 0, 0: N_SEND[None], 1: N_SEND[None] + N_SEND[0]}[side]
+            if len(mine) >= pool:
+                mine[-pool].wait_send()
             self.made().start()
-            started[side].append(self)
+            mine.append(self)
 
         def made(self):
             src, dst = self.refs()
             return pltpu.make_async_remote_copy(
-                src_ref=src, dst_ref=dst, send_sem=send.at[self.i], recv_sem=recv.at[self.i],
+                src_ref=src, dst_ref=dst, send_sem=send.at[self.j], recv_sem=recv.at[self.i],
                 device_id=self.dev, device_id_type=pl.DeviceIdType.MESH,
             )
 
@@ -158,12 +164,14 @@
 
     own = jj(xl, y)
     u_out = copy(lambda: up_ref.at[:, pl.ds(pl.multiple_of(oc * BLK, 128), BLK)], lambda: U.at[own, c], C)
-    d_out = copy(lambda: downt_ref.at[oc], lambda: D.at[:, own, c], C)
+    d_out = copy(lambda: downt_ref.at[:, :, pl.ds(pl.multiple_of(oc * BLK, 128), BLK)], lambda: D.at[:, own, c], C)
     tok_in = pltpu.make_async_copy(tok_ref, T.at[z], local.at[0])
     tok_in.start()
     u_in = pltpu.make_async_copy(up_ref.at[:, pl.ds(pl.multiple_of(c * BLK, 128), BLK)], U.at[own, c], local.at[1])
     u_in.start()
-    d_in = pltpu.make_async_copy(downt_ref.at[c], D.at[:, own, c], local.at[2])
+    d_in = pltpu.make_async_copy(
+        downt_ref.at[:, :, pl.ds(pl.multiple_of(c * BLK, 128), BLK)], D.at[:, own, c], local.at[2]
+    )
     d_in.start()
 
     tk = {}
@@ -193,7 +201,8 @@
     u_out.wait_recv()
     gu.g0()
     tok_in.wait()
-    gate = jnp.transpose(jnp.broadcast_to(gate_ref[0:1, :], (128, BLK)))
+    gate = mod_ref[2:3, pl.ds(pl.multiple_of(z * BLK, 128), BLK)]
+    gate = jnp.transpose(jnp.broadcast_to(gate, (128, BLK)))
     GATE[:, 0:128] = gate
     GATE[:, 128:256] = gate
     tt = jnp.transpose(T[z].astype(F32))
@@ -203,11 +212,12 @@
     tok_send(2)
     gu.g2()
     gu.g3()
-    tok_send(3)
-    gu.g4()
     d_in.wait()
     d_out.wait_recv()
     gd[0].g0()
+    tok_send(3)
+    gu.g4()
+    gd[1].g0()
     tk["+", 3, 0].wait_recv()
     tk["-", 3, 1].wait_recv()
 
@@ -231,12 +241,10 @@
         return carry
 
     n_out = []
-    for p in range(2):
+
+    def norm_half(p):
         lax.fori_loop(8 * p, 8 * p + 8, norm_rows, 0)
-        rows = pl.ds(128 * p, 128)
-        n_out.append(copy_same(functools.partial(lambda rows: N.at[c, :, rows], rows), C))
-
-    gu.g5()
+        n_out.append(copy_same(lambda: N.at[c, :, pl.ds(128 * p, 128)], C))
 
     def hidden(img):
         h = nn(N[img, 0], U[0].reshape(BLK, BLK))
@@ -253,17 +261,23 @@
 
         lax.fori_loop(0, SEQ // 32, act_rows, 0)
 
-    def hidden_loop(i, carry):
-        @pl.when(i == 1)
-        def _():
-            for d in n_out:
-                d.wait_recv()
-
-        hidden(lax.rem(c + i, 2))
-        return carry
-
+    norm_half(0)
     gd[0].g1()
-    lax.fori_loop(0, 2, hidden_loop, 0)
+    gd[0].g2()
+    norm_half(1)
+    gd[2].g0()
+    gu.g5()
+    gd[0].g3()
+    gd[1].g1()
+    gd[1].g2()
+    hidden(c)
+    gd[0].g4()
+    gd[3].g0()
+    gd[1].g3()
+    gd[2].g1()
+    gd[2].g2()
+    for d in n_out:
+        d.wait_recv()
 
     m_out, zs = {}, {}
 
@@ -332,7 +346,12 @@
 
             if k == 0:
                 sw[r].wait_recv()
-                vrow = valid_ref[0:1, :]
+                total = counts_ref[0]
+                for k_ in range(1, 16):
+                    total = total + counts_ref[k_]
+                norm = jnp.sqrt(jnp.full((1, SEQ), total, jnp.int32).astype(F32))
+                at = lax.broadcasted_iota(jnp.int32, (1, SEQ), 1)
+                vrow = jnp.where(at < counts_ref[dp], 1.0, 0.0) / norm
                 for h in range(2):
                     w = rows_of(r, h)
                     diff = OTA[r, h].astype(F32) - OTB[r, h].astype(F32)
@@ -365,16 +384,16 @@
             return [one(0), one(1)]
 
         def q(self, j, rows):
-            return QV[self.kind, j, :, rows]
+            return QV[self.i, j, :, rows]
 
         def r0(self):
             i, a, b = self.i, slice(0, RA), slice(RA, ROWS)
             for h in range(2):
                 for x in range(2):
-                    A2S[i, h, x] = QV[self.kind, jj(x, y2), h, a].astype(BF)
+                    A2S[i, h, x] = QV[self.i, jj(x, y2), h, a].astype(BF)
             self.a2 = self.both(A2S, A2R)
             for k in range(4):
-                XBS[i, k] = QV[self.kind, jj(xo, k), :, b].astype(BF)
+                XBS[i, k] = QV[self.i, jj(xo, k), :, b].astype(BF)
             self.xb = copy(lambda: XBS.at[i], lambda: XBR.at[i], X, 1)
 
         def r1(self):
@@ -449,7 +468,7 @@
     def down_grads(r):
         g = [GT[r, 0], GT[r, 1]]
         q = nn(g[0], ACT[0]) + nn(g[1], ACT[1])
-        QV[1] = q.reshape(NZ, 2, ROWS, BLK)
+        QV[R + r] = q.reshape(NZ, 2, ROWS, BLK)
 
     def grad_act(r):
         w = D[r].reshape(NZ * 2 * ROWS, BLK)
@@ -465,121 +484,91 @@
             for d in fw[r, k]:
                 d.wait_recv()
 
-    def transposed():
-        @pl.when(student)
-        def _():
-            def one(i, carry):
-                img, j = lax.div(i, 8), lax.rem(i, 8)
-                t = jnp.transpose(N[img, j].astype(F32)).astype(BF)
-                for r in range(R):
-                    for h in range(2):
-                        NTR[r, img, pl.ds(pl.multiple_of(j * 2 * ROWS + h * ROWS, 16), ROWS)] = t[rows_of(r, h)]
-                return carry
-
-            lax.fori_loop(0, 16, one, 0)
-
-    for r in range(R):
-        if r:
-            gd[r].g1()
-        if r > 1:
-            zstage(r - 2, 3)
-        if r + 1 < R:
-            gd[r + 1].g0()
-        if r > 0:
-            zstage(r - 1, 1)
-        if r == 1:
-            transposed()
-        gd[r].g2()
-        if r > 2:
-            output(r - 3)
-        gd[r].g3()
-        if r > 0:
-            zstage(r - 1, 2)
-        if r > 2:
-            astage(r - 3, 0)
-        gd[r].g4()
-        gd[r].g5()
-        mixed(r)
-        zstage(r, 0)
-    zstage(R - 2, 3)
-    zstage(R - 1, 1)
-    output(R - 3)
-    zstage(R - 1, 2)
-    output(R - 2)
-    astage(R - 3, 0)
-    zstage(R - 1, 3)
-    astage(0, 1)
-    output(R - 1)
-    astage(R - 2, 0)
-    astage(1, 1)
-    astage(0, 2)
-    astage(R - 1, 0)
-    astage(2, 1)
-    astage(1, 2)
-    astage(0, 3)
-    astage(3, 1)
-    astage(2, 2)
-    astage(1, 3)
-    astage(0, 4)
-    astage(3, 2)
-    astage(2, 3)
-
+    def transposed(part):
+        def one(i, carry):
+            img, j = lax.div(i, 8), lax.rem(i, 8)
+            t = jnp.transpose(N[img, j].astype(F32)).astype(BF)
+            for r in range(R):
+                for h in range(2):
+                    NTR[r, img, pl.ds(pl.multiple_of(j * 2 * ROWS + h * ROWS, 16), ROWS)] = t[rows_of(r, h)]
+            return carry
+
+        lax.fori_loop(4 * part, 4 * part + 4, one, 0)
+
+    def up_grads(r):
+        if r == 0:
+            for img in range(2):
+                GP[img] = (GA[img] * SL[img]).astype(BF)
+        q = nn(NTR[r, 0], GP[0]) + nn(NTR[r, 1], GP[1])
+        QV[r] = q.reshape(NZ, 2, ROWS, BLK)
+
+    def stage(n, k):
+        if k < 4:
+            zstage(n, k)
+        elif k == 4:
+            output(n)
+        elif k < 10:
+            astage(n, k - 5)
+        else:
+            e = red[(1, n) if n < R else (0, n - R)]
+            if k == 10:
+                if n < R:
+                    arrived(n)
+                    down_grads(n)
+                    e.r0()
+                    grad_act(n)
+                else:
+                    up_grads(n - R)
+                    e.r0()
+            elif k == 11:
+                e.r1()
+                e.r2()
+            elif k == 12:
+                e.r3()
+                e.r4()
+            elif k == 13:
+                e.r5()
+            else:
+                e.r6()
+
+    def diagonal(d):
+        for n in range(2 * R):
+            k = d - n
+            if 0 <= k < 15 and (n < R or k >= 10):
+                stage(n, k)
+
+    hidden(oc)
+    gd[0].g5()
+    mixed(0)
+    gd[1].g4()
+    gd[2].g3()
+    gd[3].g1()
+    gd[3].g2()
+    zstage(0, 0)
+    gd[1].g5()
+    mixed(1)
+    gd[2].g4()
+    gd[3].g3()
+    zstage(0, 1)
+    zstage(1, 0)
+    gd[2].g5()
+    mixed(2)
+    gd[3].g4()
+    zstage(0, 2)
+    zstage(1, 1)
+    zstage(2, 0)
+    gd[3].g5()
+    mixed(3)
+    for d in range(3, R + 4):
+        diagonal(d)
     out_ref[...] = jnp.transpose(TOKT[...]).astype(BF)
 
     @pl.when(student)
     def _():
-        arrived(0)
-        down_grads(0)
-        red[1, 0].r0()
-
-    astage(1, 4)
-    astage(3, 3)
-    astage(2, 4)
-
-    @pl.when(student)
-    def _():
-        grad_act(0)
-        red[1, 0].r1()
-        red[1, 0].r2()
-
-    astage(3, 4)
-
-    @pl.when(student)
-    def _():
-        red[1, 0].r3()
-        red[1, 0].r4()
-        order = [(1, r) for r in range(R)] + [(0, r) for r in range(R)]
-
-        def first(k, r):
-            if k == 1:
-                arrived(r)
-                down_grads(r)
-            else:
-                if r == 0:
-                    for img in range(2):
-                        GP[img] = (GA[img] * SL[img]).astype(BF)
-                q = nn(NTR[r, 0], GP[0]) + nn(NTR[r, 1], GP[1])
-                QV[0] = q.reshape(NZ, 2, ROWS, BLK)
-            red[k, r].r0()
-
-        for n in range(1, 2 * R):
-            k, r = order[n]
-            prev = red[order[n - 1]]
-            if n > 1:
-                prev.r3()
-                prev.r4()
-            prev.r5()
-            first(k, r)
-            if k == 1:
-                grad_act(r)
-            prev.r6()
-            red[k, r].r1()
-            red[k, r].r2()
-        last = red[order[-1]]
-        last.r3()
-        last.r4()
-        last.r5()
-        last.r6()
+        for d in range(R + 4, 15 + 2 * R - 1):
+            diagonal(d)
+            if d < R + 8:
+                transposed(d - R - 4)
 
     @pl.when(s == 0)
     def _():
@@ -590,29 +579,23 @@
                 for h in range(2):
                     o[ROWS * r:ROWS * (r + 1), BLK * h:BLK * (h + 1)] = HR[k * R + r, h].astype(F32)
 
-    for d in started[None]:
+    for d in started[None][-N_SEND[None]:]:
         d.wait_send()
 
     @pl.when(s == 0)
     def _():
-        for d in started[0]:
+        for d in started[0][-N_SEND[0]:]:
             d.wait_send()
 
     @pl.when(student)
     def _():
-        for d in started[1]:
+        for d in started[1][-N_SEND[1]:]:
             d.wait_send()
 
 
 def shards(axes, tokens, up_weight, down_weight, mod_table, timesteps, valid_counts):
-    mp, dp = lax.axis_index("mp"), lax.axis_index("dp")
     mod = lax.dynamic_index_in_dim(mod_table[0], timesteps[0], 0, keepdims=False)
-    gate = jnp.broadcast_to(lax.dynamic_slice_in_dim(mod[2], mp * BLK, BLK)[None], (8, BLK))
-    count = lax.dynamic_index_in_dim(valid_counts, dp, 0, keepdims=False)
-    total = jnp.sum(valid_counts).astype(F32)
-    valid = (jnp.arange(SEQ, dtype=jnp.int32) < count).astype(F32) / jnp.sqrt(total)
-    valid = jnp.broadcast_to(valid[None], (8, SEQ))
-    downt = down_weight[0].reshape(2, BLK, R, ROWS).transpose(0, 2, 3, 1)
+    downt = down_weight[0].T.reshape(R, ROWS, 2 * BLK)
 
     v = pltpu.VMEM
     nred = 2 * R
@@ -637,7 +620,7 @@
         v((R, 2, NZ * 2 * ROWS, SEQ), BF),
         v((2, SEQ, BLK), F32),
         v((2, SEQ, BLK), BF),
-        v((2, NZ, 2, ROWS, BLK), F32),
+        v((nred, NZ, 2, ROWS, BLK), F32),
         v((nred, 4, 2, ROWS - RA, BLK), BF),
         v((nred, 4, 2, ROWS - RA, BLK), BF),
         v((nred, 2, 2, RA, BLK), BF),
@@ -655,8 +638,8 @@
         v((nred, ROWS, BLK), BF),
         v((nred, 2, ROWS, BLK), BF),
         v((nred, 2, ROWS, BLK), BF),
-        pltpu.SemaphoreType.DMA((N_SEM,)),
-        pltpu.SemaphoreType.DMA((N_SEM,)),
+        pltpu.SemaphoreType.DMA((sum(N_SEND.values()),)),
+        pltpu.SemaphoreType.DMA((N_RECV,)),
         pltpu.SemaphoreType.DMA((3,)),
     ]
     hbm = pl.BlockSpec(memory_space=pl.ANY)
@@ -668,13 +651,13 @@
             jax.ShapeDtypeStruct((96, 2 * BLK), F32),
             jax.ShapeDtypeStruct((96, 2 * BLK), F32),
         ),
-        in_specs=[hbm, hbm, hbm, vm, vm, vm],
+        in_specs=[hbm, hbm, hbm, vm, pl.BlockSpec(memory_space=pltpu.SMEM)],
         out_specs=(vm, vm, vm),
         scratch_shapes=scratch,
         compiler_params=pltpu.CompilerParams(
             collective_id=0, has_side_effects=True, vmem_limit_bytes=67043328
         ),
-    )(tokens, up_weight[0], downt, mod, gate, valid)
+    )(tokens, up_weight[0], downt, mod, valid_counts)
     return out[None], up, down.T
 
 

time: 232 us -> 147 us (0.63)
  the two profiles are of different devices: /device:TPU:5 before, /device:TPU:7 now
where the time goes in v2:
time: 147 us
  Pallas kernels  139 us (95%)
  local copies, waits for them, and re-layouts  6.42 us (4%)
    pallas_call x1, Pallas kernels, shards(): pl.pallas_call(functools.partial(kernel, axes), out_shape=(jax.ShapeDtype...  139 us
    unnamed x4, local copies, waits for them, and re-layouts  5.64 us

profile of v2, /device:TPU:7, one launch (start us, length us, event | category | flops | bytes accessed | tf_op | source)
XLA Modules:
  0.0 146.5 jit_solution(4992777191962317065)
XLA Ops:
  1.3 0.8 constant_dynamic-slice_fusion
  2.1 0.6 copy.11
  2.7 138.8 %shard_map.85 = (bf16[256,384]{1,0:T(8,128)(2,1)}, f32[96,768]{1,0:T(8,128)}, f32[96,768]{1,0:T(8,128)}) custom-call(bf16[256,384]{1,0:T(8,128)(2,1)} %tok_ref.1, bf16[192,768]{1,0:T(8,128)(2,1)} %bitcast.16, bf16[4,48,768]{2,1,0:T(8,128)(2,1)} %bitcast.17, f32[3,3072]{1,0:T(4,128)} %bitcast.19, s32[16]{0:T(128)} %counts_ref.1), custom_call_target="tpu_custom_call" | custom-call | tf_op jit(solution)/shard_map/pallas_call | solution.py:647
  141.5 1.6 %copy.16 = bf16[1,256,384]{2,1,0:T(8,128)(2,1)} copy(bf16[1,256,384]{2,1,0:T(8,128)(2,1)} %bitcast.18) | data formatting | bytes 393216
  143.2 1.7 %copy.17 = f32[96,768]{1,0:T(8,128)} copy(f32[96,768]{1,0:T(8,128)} %get-tuple-element.13) | data formatting | bytes 589824
  144.9 1.7 %copy.18 = f32[768,96]{0,1:T(8,128)} copy(f32[768,96]{0,1:T(8,128)} %bitcast.15) | data formatting | bytes 589824

commit v3 on v2

--- a/solution.py
+++ b/solution.py
@@ -15,7 +15,7 @@
 NZ = 8
 SEQ = 256
 BLK = 384
-N_RECV = 290
+N_RECV = 192
 N_SEND = {None: 32, 0: 4, 1: 32}
 
 
@@ -85,9 +85,12 @@
     started = {None: [], 0: [], 1: []}
 
     class Copy:
-        def __init__(self, refs, dev, side):
-            self.refs, self.dev, self.i = refs, dev, used[0]
-            used[0] += 1
+        def __init__(self, refs, dev, side, at=None):
+            self.refs, self.dev = refs, dev
+            if at is None:
+                at = used[0]
+                used[0] += 1
+            self.i = at
             mine = started[side]
             pool = N_SEND[side]
             self.j = len(mine) % pool + {None: 0, 0: N_SEND[None], 1: N_SEND[None] + N_SEND[0]}[side]
@@ -109,23 +112,28 @@
         def wait_send(self):
             self.made().wait_send()
 
-    def copy(src, dst, dev, side=None):
-        return Copy(lambda: (src(), dst()), dev, side)
-
-    def copy_same(at, dev, side=None):
-        return Copy(lambda: (at(),) * 2, dev, side)
+    def copy(src, dst, dev, side=None, at=None):
+        return Copy(lambda: (src(), dst()), dev, side, at)
+
+    def copy_same(ref, dev, side=None, at=None):
+        return Copy(lambda: (ref(),) * 2, dev, side, at)
+
+    def wait_bytes(i, ref):
+        pltpu.make_async_copy(ref, ref, recv.at[i]).wait()
 
     student = s == 1
 
     class Gather:
-        def __init__(self, buf, ra):
-            self.buf, self.ra = buf, ra
+        def __init__(self, buf, ra, four):
+            self.buf, self.ra, self.four = buf, ra, four
 
         def g0(self):
+            self.bx = used[0]
+            used[0] += 1
             self.xa = copy_same(lambda: self.apart(xl, y), X)
             self.yp = copy_same(lambda: self.buf(own), YP)
             self.ym = copy_same(lambda: self.buf(own), YM)
-            self.xb = copy_same(lambda: self.bpart(xl, y), X)
+            self.xb = copy_same(lambda: self.bpart(xl, y), X, at=self.bx)
 
         def g1(self):
             self.xa.wait_recv()
@@ -142,10 +150,10 @@
         def g2(self):
             self.yp.wait_recv()
             self.rp = copy_same(lambda: self.buf(jj(xl, ym)).at[0], YP)
-            self.bxm = copy_same(lambda: self.bpart(xl, ym), X)
+            self.bxm = copy_same(lambda: self.bpart(xl, ym), X, at=self.bx)
             self.ym.wait_recv()
             self.rm = copy_same(lambda: self.buf(jj(xl, yp)).at[1], YM)
-            self.bxp = copy_same(lambda: self.bpart(xl, yp), X)
+            self.bxp = copy_same(lambda: self.bpart(xl, yp), X, at=self.bx)
 
         def g3(self):
             self.xap.wait_recv()
@@ -156,11 +164,12 @@
         def g4(self):
             self.rp.wait_recv()
             self.rm.wait_recv()
-            self.bx2 = copy_same(lambda: self.bpart(xl, y2), X)
+            self.bx2 = copy_same(lambda: self.bpart(xl, y2), X, at=self.bx)
 
         def g5(self):
-            for d in (self.xb, self.bxm, self.bxp, self.rxp, self.rxm, self.bx2):
-                d.wait_recv()
+            self.rxp.wait_recv()
+            self.rxm.wait_recv()
+            wait_bytes(self.bx, self.four())
 
     own = jj(xl, y)
     u_out = copy(lambda: up_ref.at[:, pl.ds(pl.multiple_of(oc * BLK, 128), BLK)], lambda: U.at[own, c], C)
@@ -193,8 +202,11 @@
             if hop < 3 or p == 1:
                 tk["-", hop, p] = copy(src, functools.partial(at, hop), ZM)
 
-    gu = Gather(lambda j: U.at[j], 128)
-    gd = [Gather(functools.partial(lambda r, j: D.at[r, j], r), RA) for r in range(R)]
+    gu = Gather(lambda j: U.at[j], 128, lambda: U.at[0:4, :, 128:192])
+    gd = [
+        Gather(functools.partial(lambda r, j: D.at[r, j], r), RA, functools.partial(lambda r: D.at[r, 0:4, :, RA:ROWS], r))
+        for r in range(R)
+    ]
 
     tok_send(0)
     u_in.wait()
@@ -211,13 +223,15 @@
     gu.g1()
     tok_send(2)
     gu.g2()
-    gu.g3()
     d_in.wait()
     d_out.wait_recv()
+    gu.g3()
     gd[0].g0()
+    gd[1].g0()
     tok_send(3)
     gu.g4()
-    gd[1].g0()
+    gd[2].g0()
+    gd[3].g0()
     tk["+", 3, 0].wait_recv()
     tk["-", 3, 1].wait_recv()
 
@@ -264,18 +278,19 @@
     norm_half(0)
     gd[0].g1()
     gd[0].g2()
-    norm_half(1)
-    gd[2].g0()
-    gu.g5()
-    gd[0].g3()
     gd[1].g1()
     gd[1].g2()
-    hidden(c)
-    gd[0].g4()
-    gd[3].g0()
-    gd[1].g3()
+    norm_half(1)
+    gu.g5()
     gd[2].g1()
     gd[2].g2()
+    gd[0].g3()
+    hidden(c)
+    gd[3].g1()
+    gd[3].g2()
+    gd[0].g4()
+    gd[1].g3()
+    gd[1].g4()
     for d in n_out:
         d.wait_recv()
 
@@ -333,6 +348,9 @@
             sw[r] = copy(lambda: OTA.at[r], lambda: OTB.at[r], S, 0)
 
     ag, fw = {}, {}
+    for r in range(R):
+        fw[r] = used[0]
+        used[0] += 1
 
     def gslice(r, img, b, h):
         n = ROWS if h is not None else 2 * ROWS
@@ -342,7 +360,7 @@
         @pl.when(student)
         def _():
             def push(kk, dev, h=None):
-                return copy_same(lambda: gslice(r, c, zz(kk), h), dev, 1)
+                return copy_same(lambda: gslice(r, c, zz(kk), h), dev, 1, fw[r] if dev is C else None)
 
             if k == 0:
                 sw[r].wait_recv()
@@ -359,27 +377,36 @@
                     GT[r, c, rows] = (GATE[w] * diff * vrow).astype(BF)
                 ag[r, 0, 0] = push(0, ZP)
                 ag[r, 1, 0] = push(0, ZM)
-                fw[r, 0] = [push(0, C)]
+                push(0, C)
                 return
             ag[r, 0, k - 1].wait_recv()
             h = 0 if k > 2 else None
             if k < 4:
                 ag[r, 0, k] = push(-k, ZP, h)
-            fw[r, k] = [push(-k, C, None if k < 4 else 0)]
+            push(-k, C, None if k < 4 else 0)
             ag[r, 1, k - 1].wait_recv()
             h = 1 if k > 2 else None
             if k < 4:
                 ag[r, 1, k] = push(k, ZM, h)
-            fw[r, k].append(push(k, C, None if k < 4 else 1))
+            push(k, C, None if k < 4 else 1)
+
+    red_sems = [[used[0] + 11 * i + j for j in range(11)] for i in range(R)]
+    used[0] += 11 * R
 
     class Reduce:
         def __init__(self, kind, r):
             self.i = kind * R + r
             self.r, self.kind = r, kind
 
-        def both(self, src, dst):
+        def sem(self, name):
+            return red_sems[self.r][self.names.index(name)]
+
+        names = ("a20", "a21", "a10", "a11", "b20", "b21", "b10", "b11", "xb", "ax", "f")
+
+        def both(self, name, src, dst):
             def one(h):
-                return copy(lambda: src.at[self.i, h], lambda: dst.at[self.i, h], (YP, YM)[h], 1)
+                at = self.sem(name + str(h))
+                return copy(lambda: src.at[self.i, h], lambda: dst.at[self.i, h], (YP, YM)[h], 1, at)
 
             return [one(0), one(1)]
 
@@ -391,10 +418,10 @@
             for h in range(2):
                 for x in range(2):
                     A2S[i, h, x] = QV[self.i, jj(x, y2), h, a].astype(BF)
-            self.a2 = self.both(A2S, A2R)
+            self.a2 = self.both("a2", A2S, A2R)
             for k in range(4):
                 XBS[i, k] = QV[self.i, jj(xo, k), :, b].astype(BF)
-            self.xb = copy(lambda: XBS.at[i], lambda: XBR.at[i], X, 1)
+            self.xb = copy(lambda: XBS.at[i], lambda: XBR.at[i], X, 1, self.sem("xb"))
 
         def r1(self):
             i, a = self.i, slice(0, RA)
@@ -404,32 +431,32 @@
                     v = self.q(jj(x, (yp, ym)[h]), a)
                     A1S[i, h, x, h] = (v[h] + A2R[i, h, x].astype(F32)).astype(BF)
                     A1S[i, h, x, 1 - h] = v[1 - h].astype(BF)
-            self.a1 = self.both(A1S, A1R)
+            self.a1 = self.both("a1", A1S, A1R)
 
         def r2(self):
             i, b = self.i, slice(RA, ROWS)
             self.xb.wait_recv()
             v = self.q(jj(xl, y2), b) + XBR[i, y2].astype(F32)
             B2S[i] = v.astype(BF)
-            self.b2 = self.both(B2S, B2R)
+            self.b2 = self.both("b2", B2S, B2R)
 
         def r3(self):
             i, b = self.i, slice(RA, ROWS)
+            for h in range(2):
+                self.a1[h].wait_recv()
             for h in range(2):
                 self.b2[h].wait_recv()
                 yy = (yp, ym)[h]
                 v = self.q(jj(xl, yy), b) + XBR[i, yy].astype(F32)
                 B1S[i, h, h] = (v[h] + B2R[i, h].astype(F32)).astype(BF)
                 B1S[i, h, 1 - h] = v[1 - h].astype(BF)
-            self.b1 = self.both(B1S, B1R)
+            self.b1 = self.both("b1", B1S, B1R)
 
         def r4(self):
             i, a = self.i, slice(0, RA)
-            for h in range(2):
-                self.a1[h].wait_recv()
             v = self.q(jj(xo, y), a) + A1R[i, 0, xo].astype(F32) + A1R[i, 1, xo].astype(F32)
             AXS[i] = v.astype(BF)
-            self.ax = copy(lambda: AXS.at[i], lambda: AXR.at[i], X, 1)
+            self.ax = copy(lambda: AXS.at[i], lambda: AXR.at[i], X, 1, self.sem("ax"))
 
         def r5(self):
             i, a, b = self.i, slice(0, RA), slice(RA, ROWS)
@@ -440,7 +467,7 @@
             FO[i, :, a] = va
             FO[i, :, b] = vb
             FS[i] = FO[i, oc].astype(BF)
-            self.f = copy(lambda: FS.at[i], lambda: FR.at[i], C, 1)
+            self.f = copy(lambda: FS.at[i], lambda: FR.at[i], C, 1, self.sem("f"))
 
         def r6(self):
             i = self.i
@@ -480,9 +507,7 @@
                 GA[img] += v
 
     def arrived(r):
-        for k in range(5):
-            for d in fw[r, k]:
-                d.wait_recv()
+        wait_bytes(fw[r], GT.at[r, 0])
 
     def transposed(part):
         def one(i, carry):
@@ -532,33 +557,28 @@
                 e.r6()
 
     def diagonal(d):
-        for n in range(2 * R):
+        for n in reversed(range(2 * R)):
             k = d - n
             if 0 <= k < 15 and (n < R or k >= 10):
                 stage(n, k)
 
     hidden(oc)
+    gd[2].g3()
+    gd[2].g4()
     gd[0].g5()
     mixed(0)
-    gd[1].g4()
-    gd[2].g3()
-    gd[3].g1()
-    gd[3].g2()
-    zstage(0, 0)
+    gd[3].g3()
+    gd[3].g4()
     gd[1].g5()
     mixed(1)
-    gd[2].g4()
-    gd[3].g3()
-    zstage(0, 1)
-    zstage(1, 0)
+    zstage(0, 0)
     gd[2].g5()
     mixed(2)
-    gd[3].g4()
-    zstage(0, 2)
-    zstage(1, 1)
-    zstage(2, 0)
+    zstage(1, 0)
+    zstage(0, 1)
     gd[3].g5()
     mixed(3)
+    diagonal(2)
     for d in range(3, R + 4):
         diagonal(d)
     out_ref[...] = jnp.transpose(TOKT[...]).astype(BF)
@@ -658,6 +678,21 @@
             collective_id=0, has_side_effects=True, vmem_limit_bytes=67043328
         ),
     )(tokens, up_weight[0], downt, mod, valid_counts)
+    def settle(out_in, up_in, down_in, out_to, up_to, down_to):
+        out_to[...] = out_in[...]
+        up_to[...] = up_in[...]
+        down_to[...] = down_in[...]
+
+    out, up, down = pl.pallas_call(
+        settle,
+        out_shape=(
+            jax.ShapeDtypeStruct((SEQ, BLK), BF),
+            jax.ShapeDtypeStruct((96, 2 * BLK), F32),
+            jax.ShapeDtypeStruct((96, 2 * BLK), F32),
+        ),
+        in_specs=[vm] * 3,
+        out_specs=(vm,) * 3,
+    )(out, up, down)
     return out[None], up, down.T
 
 

time: 147 us -> 130 us (0.88)
  the two profiles are of different devices: /device:TPU:7 before, /device:TPU:1 now
where the time goes in v3:
time: 130 us; the launch traced here: 129 us
  Pallas kernels  126 us (97%)
  local copies, waits for them, and re-layouts  1.41 us (1%)
    pallas_call x1, Pallas kernels, shards(): pl.pallas_call(functools.partial(kernel, axes), out_shape=(jax.ShapeDtype...  124 us

profile of v3, /device:TPU:1, one launch (start us, length us, event | category | flops | bytes accessed | tf_op | source)
XLA Modules:
  0.0 128.7 jit_solution(11812759998164680144)
XLA Ops:
  1.3 0.8 constant_dynamic-slice_fusion
  2.1 0.6 copy.11
  2.7 124.0 %shard_map.85 = (bf16[256,384]{1,0:T(8,128)(2,1)}, f32[96,768]{1,0:T(8,128)}, f32[96,768]{1,0:T(8,128)}) custom-call(bf16[256,384]{1,0:T(8,128)(2,1)} %tok_ref.1, bf16[192,768]{1,0:T(8,128)(2,1)} %bitcast.15, bf16[4,48,768]{2,1,0:T(8,128)(2,1)} %bitcast.16, f32[3,3072]{1,0:T(4,128)} %bitcast.17, s32[16]{0:T(128)} %counts_ref.1), custom_call_target="tpu_custom_call" | custom-call | tf_op jit(solution)/shard_map/pallas_call | solution.py:667
  126.7 2.0 %shard_map.86 = (bf16[256,384]{1,0:T(8,128)(2,1)}, f32[96,768]{1,0:T(8,128)}, f32[96,768]{1,0:T(8,128)}) custom-call(bf16[256,384]{1,0:T(8,128)(2,1)} %get-tuple-element.9.out_in, f32[96,768]{1,0:T(8,128)} %get-tuple-element.10.up_in, f32[96,768]{1,0:T(8,128)} %get-tuple-element.11.down_in), custom_call_target="tpu_custom_call" | custom-call | tf_op jit(solution)/shard_map/pallas_call | solution.py:686

commit v4 on v3

--- a/solution.py
+++ b/solution.py
@@ -11,12 +11,13 @@
 F32 = jnp.float32
 R = 4
 ROWS = 192 // R
-RA = 32
+RA = (32, 32, 32, 16)
+RU = 112
 NZ = 8
 SEQ = 256
 BLK = 384
-N_RECV = 192
-N_SEND = {None: 32, 0: 4, 1: 32}
+N_RECV = 145
+N_SEND = {None: 40, 1: 2}
 
 
 def gelu_pair(v):
@@ -45,7 +46,7 @@
     axes,
     tok_ref, up_ref, downt_ref, mod_ref, counts_ref,
     out_ref, ug_ref, dg_ref,
-    T, U, D, N, NTR, HP, SL, ACT, PO, PS, PR, ZS, ZR, GATE, TOKT, OTA, OTB, GT, GA, GP,
+    T, U, D, N, NTR, HP, SL, ACT, ACTG, PO, PS, PR, ZS, ZR, MODO, GATE, GATEG, TOKT, OTA, OTB, GT, GA, GP,
     QV, XBS, XBR, A2S, A2R, A1S, A1R, B2S, B2R, B1S, B1R, AXS, AXR, FS, FO, FR, HS, HR,
     send, recv, local,
 ):
@@ -82,7 +83,7 @@
     pl.semaphore_wait(barrier, len(peers))
 
     used = [0]
-    started = {None: [], 0: [], 1: []}
+    started = {None: [], 1: []}
 
     class Copy:
         def __init__(self, refs, dev, side, at=None):
@@ -93,7 +94,7 @@
             self.i = at
             mine = started[side]
             pool = N_SEND[side]
-            self.j = len(mine) % pool + {None: 0, 0: N_SEND[None], 1: N_SEND[None] + N_SEND[0]}[side]
+            self.j = len(mine) % pool + {None: 0, 1: N_SEND[None]}[side]
             if len(mine) >= pool:
                 mine[-pool].wait_send()
             self.made().start()
@@ -202,13 +203,17 @@
             if hop < 3 or p == 1:
                 tk["-", hop, p] = copy(src, functools.partial(at, hop), ZM)
 
-    gu = Gather(lambda j: U.at[j], 128, lambda: U.at[0:4, :, 128:192])
+    gu = Gather(lambda j: U.at[j], RU, lambda: U.at[0:4, :, RU:192])
     gd = [
-        Gather(functools.partial(lambda r, j: D.at[r, j], r), RA, functools.partial(lambda r: D.at[r, 0:4, :, RA:ROWS], r))
+        Gather(
+            functools.partial(lambda r, j: D.at[r, j], r), RA[r],
+            functools.partial(lambda r: D.at[r, 0:4, :, RA[r]:ROWS], r),
+        )
         for r in range(R)
     ]
 
     tok_send(0)
+    mod_out = copy(lambda: mod_ref, lambda: MODO, S)
     u_in.wait()
     u_out.wait_recv()
     gu.g0()
@@ -217,6 +222,15 @@
     gate = jnp.transpose(jnp.broadcast_to(gate, (128, BLK)))
     GATE[:, 0:128] = gate
     GATE[:, 128:256] = gate
+
+    def gate_of_student():
+        mod_out.wait_recv()
+        at = pl.ds(pl.multiple_of(z * BLK, 128), BLK)
+        g = jnp.where(jnp.full((1, BLK), s) == 1, mod_ref[2:3, at], MODO[2:3, at])
+        g = jnp.transpose(jnp.broadcast_to(g, (128, BLK)))
+        GATEG[:, 0:128] = g
+        GATEG[:, 128:256] = g
+
     tt = jnp.transpose(T[z].astype(F32))
     TOKT[...] = tt
     tok_send(1)
@@ -227,11 +241,9 @@
     d_out.wait_recv()
     gu.g3()
     gd[0].g0()
-    gd[1].g0()
     tok_send(3)
     gu.g4()
-    gd[2].g0()
-    gd[3].g0()
+    gd[1].g0()
     tk["+", 3, 0].wait_recv()
     tk["-", 3, 1].wait_recv()
 
@@ -275,26 +287,39 @@
 
         lax.fori_loop(0, SEQ // 32, act_rows, 0)
 
+    act_out = []
+
+    def send_act(img):
+        @pl.when(student)
+        def _():
+            act_out.append(copy(lambda: ACT.at[img()], lambda: ACTG.at[img()], S, 1))
+
     norm_half(0)
     gd[0].g1()
     gd[0].g2()
+    norm_half(1)
+    gu.g5()
+    gd[2].g0()
     gd[1].g1()
     gd[1].g2()
-    norm_half(1)
-    gu.g5()
+    gd[0].g3()
+    hidden(c)
+    send_act(lambda: c)
+    gd[0].g4()
+    gd[3].g0()
     gd[2].g1()
     gd[2].g2()
-    gd[0].g3()
-    hidden(c)
-    gd[3].g1()
-    gd[3].g2()
-    gd[0].g4()
     gd[1].g3()
-    gd[1].g4()
     for d in n_out:
         d.wait_recv()
 
     m_out, zs = {}, {}
+    z_sems = used[0]
+    used[0] += 4 * R
+
+    def ring(r, q, k):
+        return z_sems + 4 * r + 2 * q + k % 2
+
 
     def mixed(r):
         w = D[r].reshape(NZ * 2 * ROWS, BLK)
@@ -312,11 +337,12 @@
             m_out[r].wait_recv()
             v = val(r, zz(4)).astype(BF)
             ZS[r, 0, 0] = v
-            zs[r, 0, 0] = copy(lambda: ZS.at[r, 0, 0, h0], lambda: ZR.at[r, 0, 0, h0], ZP)
-            zs[r, 1, 0] = copy(lambda: ZS.at[r, 0, 0, h1], lambda: ZR.at[r, 1, 0, h1], ZM)
+            zs[r, 0, 0] = copy(lambda: ZS.at[r, 0, 0, h0], lambda: ZR.at[r, 0, 0, h0], ZP, None, ring(r, 0, 0))
+            zs[r, 1, 0] = copy(lambda: ZS.at[r, 0, 0, h1], lambda: ZR.at[r, 1, 0, h1], ZM, None, ring(r, 1, 0))
             return
         for q in range(2):
             zs[r, q, k - 1].wait_recv()
+        for q in range(2):
             v = val(r, zz((4 - k) if q == 0 else (k - 4)))
             if k == 1:
                 h = slice(0, ROWS) if q == 0 else slice(ROWS, 2 * ROWS)
@@ -326,7 +352,8 @@
             else:
                 ZS[r, q, k] = (v + ZR[r, q, k - 1].astype(F32)).astype(BF)
             at = functools.partial(lambda ref, q: ref.at[r, q, k], q=q)
-            zs[r, q, k] = copy(functools.partial(at, ZS), functools.partial(at, ZR), ZP if q == 0 else ZM)
+            to = ZP if q == 0 else ZM
+            zs[r, q, k] = copy(functools.partial(at, ZS), functools.partial(at, ZR), to, None, ring(r, q, k))
 
     sw = {}
 
@@ -343,9 +370,7 @@
             OTA[r, h] = o
             TOKT[w] = o.astype(F32)
 
-        @pl.when(s == 0)
-        def _():
-            sw[r] = copy(lambda: OTA.at[r], lambda: OTB.at[r], S, 0)
+        sw[r] = copy(lambda: OTA.at[r], lambda: OTB.at[r], S)
 
     ag, fw = {}, {}
     for r in range(R):
@@ -357,145 +382,144 @@
         return GT.at[r, img, pl.ds(pl.multiple_of(b * 2 * ROWS + (h or 0) * ROWS, 16), n)]
 
     def astage(r, k):
-        @pl.when(student)
-        def _():
-            def push(kk, dev, h=None):
-                return copy_same(lambda: gslice(r, c, zz(kk), h), dev, 1, fw[r] if dev is C else None)
-
-            if k == 0:
-                sw[r].wait_recv()
-                total = counts_ref[0]
-                for k_ in range(1, 16):
-                    total = total + counts_ref[k_]
-                norm = jnp.sqrt(jnp.full((1, SEQ), total, jnp.int32).astype(F32))
-                at = lax.broadcasted_iota(jnp.int32, (1, SEQ), 1)
-                vrow = jnp.where(at < counts_ref[dp], 1.0, 0.0) / norm
-                for h in range(2):
-                    w = rows_of(r, h)
-                    diff = OTA[r, h].astype(F32) - OTB[r, h].astype(F32)
-                    rows = pl.ds(pl.multiple_of(z * 2 * ROWS + h * ROWS, 16), ROWS)
-                    GT[r, c, rows] = (GATE[w] * diff * vrow).astype(BF)
-                ag[r, 0, 0] = push(0, ZP)
-                ag[r, 1, 0] = push(0, ZM)
-                push(0, C)
-                return
-            ag[r, 0, k - 1].wait_recv()
-            h = 0 if k > 2 else None
-            if k < 4:
-                ag[r, 0, k] = push(-k, ZP, h)
-            push(-k, C, None if k < 4 else 0)
-            ag[r, 1, k - 1].wait_recv()
-            h = 1 if k > 2 else None
-            if k < 4:
-                ag[r, 1, k] = push(k, ZM, h)
-            push(k, C, None if k < 4 else 1)
-
-    red_sems = [[used[0] + 11 * i + j for j in range(11)] for i in range(R)]
-    used[0] += 11 * R
+        def push(kk, dev, h=None, at=None):
+            return copy_same(lambda: gslice(r, c, zz(kk), h), dev, None, fw[r] if at is None else at)
+
+        if k == 0:
+            sw[r].wait_recv()
+            total = counts_ref[0]
+            for i in range(1, 16):
+                total = total + counts_ref[i]
+            norm = jnp.sqrt(jnp.full((1, SEQ), total, jnp.int32).astype(F32))
+            at = lax.broadcasted_iota(jnp.int32, (1, SEQ), 1)
+            vrow = jnp.where(at < counts_ref[dp], (2 * s - 1).astype(F32), 0.0) / norm
+            for h in range(2):
+                w = rows_of(r, h)
+                diff = OTA[r, h].astype(F32) - OTB[r, h].astype(F32)
+                rows = pl.ds(pl.multiple_of(z * 2 * ROWS + h * ROWS, 16), ROWS)
+                GT[r, c, rows] = (GATEG[w] * diff * vrow).astype(BF)
+            ag[r, 0, 0] = push(0, ZP, at=ring(r, 0, 4))
+            ag[r, 1, 0] = push(0, ZM, at=ring(r, 1, 4))
+            push(0, C)
+            return
+        ag[r, 0, k - 1].wait_recv()
+        ag[r, 1, k - 1].wait_recv()
+        if k < 4:
+            ag[r, 0, k] = push(-k, ZP, 0 if k > 2 else None, ring(r, 0, 4 + k))
+        push(-k, C, None if k < 4 else 0)
+        if k < 4:
+            ag[r, 1, k] = push(k, ZM, 1 if k > 2 else None, ring(r, 1, 4 + k))
+        push(k, C, None if k < 4 else 1)
 
     class Reduce:
-        def __init__(self, kind, r):
-            self.i = kind * R + r
-            self.r, self.kind = r, kind
-
-        def sem(self, name):
-            return red_sems[self.r][self.names.index(name)]
-
-        names = ("a20", "a21", "a10", "a11", "b20", "b21", "b10", "b11", "xb", "ax", "f")
-
-        def both(self, name, src, dst):
+        def __init__(self, i):
+            self.i, self.a, self.b = i, slice(0, RA[i]), slice(RA[i], ROWS)
+            self.ra, self.rb = pl.ds(0, RA[i]), pl.ds(0, ROWS - RA[i])
+            self.r = lax.rem(i + 2 * (1 - s), R)
+
+        def both(self, src, dst):
             def one(h):
-                at = self.sem(name + str(h))
-                return copy(lambda: src.at[self.i, h], lambda: dst.at[self.i, h], (YP, YM)[h], 1, at)
+                return copy(lambda: src().at[h], lambda: dst().at[h], (YP, YM)[h])
 
             return [one(0), one(1)]
 
         def q(self, j, rows):
-            return QV[self.i, j, :, rows]
+            return QV[self.r, j, :, rows]
 
         def r0(self):
-            i, a, b = self.i, slice(0, RA), slice(RA, ROWS)
+            i, ra, rb = self.i, self.ra, self.rb
             for h in range(2):
                 for x in range(2):
-                    A2S[i, h, x] = QV[self.i, jj(x, y2), h, a].astype(BF)
-            self.a2 = self.both("a2", A2S, A2R)
+                    A2S[i, h, x, ra] = QV[self.r, jj(x, y2), h, self.a].astype(BF)
+            self.a2 = self.both(lambda: A2S.at[i, :, :, ra], lambda: A2R.at[i, :, :, ra])
             for k in range(4):
-                XBS[i, k] = QV[self.i, jj(xo, k), :, b].astype(BF)
-            self.xb = copy(lambda: XBS.at[i], lambda: XBR.at[i], X, 1, self.sem("xb"))
+                XBS[i, k, :, rb] = self.q(jj(xo, k), self.b).astype(BF)
+            self.xb = copy(lambda: XBS.at[i, :, :, rb], lambda: XBR.at[i, :, :, rb], X)
 
         def r1(self):
-            i, a = self.i, slice(0, RA)
+            i, ra = self.i, self.ra
             for h in range(2):
                 self.a2[h].wait_recv()
                 for x in range(2):
-                    v = self.q(jj(x, (yp, ym)[h]), a)
-                    A1S[i, h, x, h] = (v[h] + A2R[i, h, x].astype(F32)).astype(BF)
-                    A1S[i, h, x, 1 - h] = v[1 - h].astype(BF)
-            self.a1 = self.both("a1", A1S, A1R)
+                    v = self.q(jj(x, (yp, ym)[h]), self.a)
+                    A1S[i, h, x, h, ra] = (v[h] + A2R[i, h, x, ra].astype(F32)).astype(BF)
+                    A1S[i, h, x, 1 - h, ra] = v[1 - h].astype(BF)
+            self.a1 = self.both(lambda: A1S.at[i, :, :, :, ra], lambda: A1R.at[i, :, :, :, ra])
 
         def r2(self):
-            i, b = self.i, slice(RA, ROWS)
+            i, rb = self.i, self.rb
             self.xb.wait_recv()
-            v = self.q(jj(xl, y2), b) + XBR[i, y2].astype(F32)
-            B2S[i] = v.astype(BF)
-            self.b2 = self.both("b2", B2S, B2R)
+            v = self.q(jj(xl, y2), self.b) + XBR[i, y2, :, rb].astype(F32)
+            B2S[i, :, rb] = v.astype(BF)
+            self.b2 = self.both(lambda: B2S.at[i, :, rb], lambda: B2R.at[i, :, rb])
 
         def r3(self):
-            i, b = self.i, slice(RA, ROWS)
-            for h in range(2):
-                self.a1[h].wait_recv()
+            i, rb = self.i, self.rb
             for h in range(2):
                 self.b2[h].wait_recv()
                 yy = (yp, ym)[h]
-                v = self.q(jj(xl, yy), b) + XBR[i, yy].astype(F32)
-                B1S[i, h, h] = (v[h] + B2R[i, h].astype(F32)).astype(BF)
-                B1S[i, h, 1 - h] = v[1 - h].astype(BF)
-            self.b1 = self.both("b1", B1S, B1R)
+                v = self.q(jj(xl, yy), self.b) + XBR[i, yy, :, rb].astype(F32)
+                B1S[i, h, h, rb] = (v[h] + B2R[i, h, rb].astype(F32)).astype(BF)
+                B1S[i, h, 1 - h, rb] = v[1 - h].astype(BF)
+            self.b1 = self.both(lambda: B1S.at[i, :, :, rb], lambda: B1R.at[i, :, :, rb])
 
         def r4(self):
-            i, a = self.i, slice(0, RA)
-            v = self.q(jj(xo, y), a) + A1R[i, 0, xo].astype(F32) + A1R[i, 1, xo].astype(F32)
-            AXS[i] = v.astype(BF)
-            self.ax = copy(lambda: AXS.at[i], lambda: AXR.at[i], X, 1, self.sem("ax"))
+            i, ra = self.i, self.ra
+            for h in range(2):
+                self.a1[h].wait_recv()
+            v = self.q(jj(xo, y), self.a) + A1R[i, 0, xo, :, ra].astype(F32) + A1R[i, 1, xo, :, ra].astype(F32)
+            AXS[i, :, ra] = v.astype(BF)
+            self.ax = copy(lambda: AXS.at[i, :, ra], lambda: AXR.at[i, :, ra], X)
 
         def r5(self):
-            i, a, b = self.i, slice(0, RA), slice(RA, ROWS)
-            for d in (self.ax, *self.b1):
+            i, ra, rb = self.i, self.ra, self.rb
+            va = self.q(own, self.a) + A1R[i, 0, xl, :, ra].astype(F32) + A1R[i, 1, xl, :, ra].astype(F32)
+            vb = self.q(own, self.b) + XBR[i, y, :, rb].astype(F32)
+            for d in self.b1:
                 d.wait_recv()
-            va = self.q(own, a) + A1R[i, 0, xl].astype(F32) + A1R[i, 1, xl].astype(F32) + AXR[i].astype(F32)
-            vb = self.q(own, b) + XBR[i, y].astype(F32) + B1R[i, 0].astype(F32) + B1R[i, 1].astype(F32)
-            FO[i, :, a] = va
-            FO[i, :, b] = vb
+            vb = vb + B1R[i, 0, :, rb].astype(F32) + B1R[i, 1, :, rb].astype(F32)
+            self.ax.wait_recv()
+            FO[i, :, self.a] = va + AXR[i, :, ra].astype(F32)
+            FO[i, :, self.b] = vb
             FS[i] = FO[i, oc].astype(BF)
-            self.f = copy(lambda: FS.at[i], lambda: FR.at[i], C, 1, self.sem("f"))
+            self.f = copy(lambda: FS.at[i], lambda: FR.at[i], C)
 
         def r6(self):
             i = self.i
             self.f.wait_recv()
-            if self.r < R // 2:
+            if i < R // 2:
                 HS[i, c] = FO[i, c].astype(BF)
                 HS[i, oc] = FR[i]
-                self.h = copy(lambda: HS.at[i], lambda: HR.at[i], S, 1)
-            else:
-                o = (ug_ref, dg_ref)[self.kind]
-                rows = slice(ROWS * (self.r - R // 2), ROWS * (self.r - R // 2 + 1))
-
-                @pl.when(c == 0)
-                def _():
-                    o[rows, 0:BLK] = FO[i, 0]
-                    o[rows, BLK:2 * BLK] = FR[i].astype(F32)
-
-                @pl.when(c == 1)
-                def _():
-                    o[rows, 0:BLK] = FR[i].astype(F32)
-                    o[rows, BLK:2 * BLK] = FO[i, 1]
-
-    red = {(k, r): Reduce(k, r) for k in range(2) for r in range(R)}
+                self.h = copy(lambda: HS.at[i], lambda: HR.at[i], S)
+                return
+            FO[i, oc] = FR[i].astype(F32)
+            rows = slice(ROWS * (i - R // 2), ROWS * (i - R // 2 + 1))
+
+            def keep(o):
+                for h in range(2):
+                    o[rows, BLK * h:BLK * (h + 1)] = FO[i, h]
+
+            pl.when(student)(lambda: keep(ug_ref))
+            pl.when(s == 0)(lambda: keep(dg_ref))
+
+        def r7(self):
+            i = self.i
+            self.h.wait_recv()
+            rows = slice(ROWS * i, ROWS * (i + 1))
+
+            def keep(o):
+                for h in range(2):
+                    o[rows, BLK * h:BLK * (h + 1)] = HR[i, h].astype(F32)
+
+            pl.when(student)(lambda: keep(dg_ref))
+            pl.when(s == 0)(lambda: keep(ug_ref))
+
+    red = [Reduce(i) for i in range(R)]
 
     def down_grads(r):
         g = [GT[r, 0], GT[r, 1]]
-        q = nn(g[0], ACT[0]) + nn(g[1], ACT[1])
-        QV[R + r] = q.reshape(NZ, 2, ROWS, BLK)
+        q = nn(g[0], ACTG[0]) + nn(g[1], ACTG[1])
+        QV[r] = q.reshape(NZ, 2, ROWS, BLK)
 
     def grad_act(r):
         w = D[r].reshape(NZ * 2 * ROWS, BLK)
@@ -535,77 +559,82 @@
         elif k < 10:
             astage(n, k - 5)
         else:
-            e = red[(1, n) if n < R else (0, n - R)]
-            if k == 10:
-                if n < R:
-                    arrived(n)
-                    down_grads(n)
-                    e.r0()
-                    grad_act(n)
-                else:
-                    up_grads(n - R)
-                    e.r0()
-            elif k == 11:
-                e.r1()
-                e.r2()
-            elif k == 12:
-                e.r3()
-                e.r4()
-            elif k == 13:
-                e.r5()
-            else:
-                e.r6()
+            arrived(n)
+            pl.when(student)(lambda: grad_act(n))
+
+            @pl.when(s == 0)
+            def _():
+                if n == 0:
+                    for d in act_out:
+                        d.wait_recv()
+                down_grads(n)
 
     def diagonal(d):
-        for n in reversed(range(2 * R)):
+        for n in reversed(range(R)):
             k = d - n
-            if 0 <= k < 15 and (n < R or k >= 10):
+            if 0 <= k < 11:
                 stage(n, k)
 
     hidden(oc)
-    gd[2].g3()
-    gd[2].g4()
+    send_act(lambda: oc)
     gd[0].g5()
     mixed(0)
-    gd[3].g3()
-    gd[3].g4()
+    gd[3].g1()
+    gd[3].g2()
+    gd[1].g4()
+    gd[2].g3()
+    zstage(0, 0)
     gd[1].g5()
     mixed(1)
-    zstage(0, 0)
+    gd[2].g4()
+    gd[3].g3()
+    zstage(0, 1)
+    zstage(1, 0)
     gd[2].g5()
     mixed(2)
-    zstage(1, 0)
-    zstage(0, 1)
+    gd[3].g4()
+    gate_of_student()
     gd[3].g5()
     mixed(3)
     diagonal(2)
     for d in range(3, R + 4):
         diagonal(d)
     out_ref[...] = jnp.transpose(TOKT[...]).astype(BF)
-
-    @pl.when(student)
-    def _():
-        for d in range(R + 4, 15 + 2 * R - 1):
-            diagonal(d)
-            if d < R + 8:
-                transposed(d - R - 4)
-
-    @pl.when(s == 0)
-    def _():
-        for k in (1, 0):
-            o = (ug_ref, dg_ref)[k]
-            for r in range(R // 2):
-                red[k, r].h.wait_recv()
-                for h in range(2):
-                    o[ROWS * r:ROWS * (r + 1), BLK * h:BLK * (h + 1)] = HR[k * R + r, h].astype(F32)
+    for d in range(R + 4, 11 + R - 1):
+        diagonal(d)
+        if d < R + 8:
+            pl.when(student)(lambda: transposed(d - R - 4))
+
+    def begin(n):
+        pl.when(student)(lambda: up_grads(n))
+        red[n].r0()
+
+    def rstage(n, k):
+        if k == 0:
+            begin(n)
+        elif k == 1:
+            red[n].r1()
+            red[n].r2()
+        elif k == 2:
+            red[n].r3()
+            red[n].r4()
+        elif k == 3:
+            red[n].r5()
+        else:
+            red[n].r6()
+
+    begin(0)
+    begin(1)
+    for d in range(2, R + 5):
+        for n in reversed(range(R)):
+            k = d - n if d - n < 1 else d - n - 1
+            if d - n == 0 and n > 1 or 1 <= k < 5 and d - n > 1:
+                rstage(n, k)
+    for n in range(R // 2):
+        red[n].r7()
 
     for d in started[None][-N_SEND[None]:]:
         d.wait_send()
-
-    @pl.when(s == 0)
-    def _():
-        for d in started[0][-N_SEND[0]:]:
-            d.wait_send()
 
     @pl.when(student)
     def _():
@@ -618,7 +647,7 @@
     downt = down_weight[0].T.reshape(R, ROWS, 2 * BLK)
 
     v = pltpu.VMEM
-    nred = 2 * R
+    nred = R
     scratch = [
         v((NZ, SEQ, BLK), BF),
         v((NZ, 2, 192, BLK), BF),
@@ -628,11 +657,14 @@
         v((SEQ, BLK), F32),
         v((2, SEQ, BLK), F32),
         v((2, SEQ, BLK), BF),
+        v((2, SEQ, BLK), BF),
         v((R, NZ * 2 * ROWS, SEQ), F32),
         v((R, NZ * 2 * ROWS, SEQ), BF),
         v((R, NZ * 2 * ROWS, SEQ), BF),
         v((R, 2, 4, 2 * ROWS, SEQ), BF),
         v((R, 2, 4, 2 * ROWS, SEQ), BF),
+        v((3, NZ * BLK), F32),
+        v((BLK, SEQ), F32),
         v((BLK, SEQ), F32),
         v((BLK, SEQ), F32),
         v((R, 2, ROWS, SEQ), BF),
@@ -641,18 +673,18 @@
         v((2, SEQ, BLK), F32),
         v((2, SEQ, BLK), BF),
         v((nred, NZ, 2, ROWS, BLK), F32),
-        v((nred, 4, 2, ROWS - RA, BLK), BF),
-        v((nred, 4, 2, ROWS - RA, BLK), BF),
-        v((nred, 2, 2, RA, BLK), BF),
-        v((nred, 2, 2, RA, BLK), BF),
-        v((nred, 2, 2, 2, RA, BLK), BF),
-        v((nred, 2, 2, 2, RA, BLK), BF),
-        v((nred, 2, ROWS - RA, BLK), BF),
-        v((nred, 2, ROWS - RA, BLK), BF),
-        v((nred, 2, 2, ROWS - RA, BLK), BF),
-        v((nred, 2, 2, ROWS - RA, BLK), BF),
-        v((nred, 2, RA, BLK), BF),
-        v((nred, 2, RA, BLK), BF),
+        v((nred, 4, 2, 32, BLK), BF),
+        v((nred, 4, 2, 32, BLK), BF),
+        v((nred, 2, 2, 32, BLK), BF),
+        v((nred, 2, 2, 32, BLK), BF),
+        v((nred, 2, 2, 2, 32, BLK), BF),
+        v((nred, 2, 2, 2, 32, BLK), BF),
+        v((nred, 2, 32, BLK), BF),
+        v((nred, 2, 32, BLK), BF),
+        v((nred, 2, 2, 32, BLK), BF),
+        v((nred, 2, 2, 32, BLK), BF),
+        v((nred, 2, 32, BLK), BF),
+        v((nred, 2, 32, BLK), BF),
         v((nred, ROWS, BLK), BF),
         v((nred, 2, ROWS, BLK), F32),
         v((nred, ROWS, BLK), BF),

time: 130 us -> 131 us (level)
  Pallas kernels: 126 us -> 128 us
    pallas_call x1, Pallas kernels: 124 us -> 126 us  [shards(): pl.pallas_call(functools.partial(kernel, axes), out_shape=(jax.ShapeDtype...]
where the time goes in v4:
time: 131 us
  Pallas kernels  128 us (98%)
  local copies, waits for them, and re-layouts  1.41 us (1%)
    pallas_call x1, Pallas kernels, shards(): pl.pallas_call(functools.partial(kernel, axes), out_shape=(jax.ShapeDtype...  126 us

profile of v4, /device:TPU:1, one launch (start us, length us, event | category | flops | bytes accessed | tf_op | source)
XLA Modules:
  0.0 130.6 jit_solution(1767157000545207515)
XLA Ops:
  1.3 0.8 constant_dynamic-slice_fusion
  2.1 0.6 copy.11
  2.7 125.9 %shard_map.85 = (bf16[256,384]{1,0:T(8,128)(2,1)}, f32[96,768]{1,0:T(8,128)}, f32[96,768]{1,0:T(8,128)}) custom-call(bf16[256,384]{1,0:T(8,128)(2,1)} %tok_ref.1, bf16[192,768]{1,0:T(8,128)(2,1)} %bitcast.15, bf16[4,48,768]{2,1,0:T(8,128)(2,1)} %bitcast.16, f32[3,3072]{1,0:T(4,128)} %bitcast.17, s32[16]{0:T(128)} %counts_ref.1), custom_call_target="tpu_custom_call" | custom-call | tf_op jit(solution)/shard_map/pallas_call | solution.py:699
  128.6 2.0 %shard_map.86 = (bf16[256,384]{1,0:T(8,128)(2,1)}, f32[96,768]{1,0:T(8,128)}, f32[96,768]{1,0:T(8,128)}) custom-call(bf16[256,384]{1,0:T(8,128)(2,1)} %get-tuple-element.9.out_in, f32[96,768]{1,0:T(8,128)} %get-tuple-element.10.up_in, f32[96,768]{1,0:T(8,128)} %get-tuple-element.11.down_in), custom_call_target="tpu_custom_call" | custom-call | tf_op jit(solution)/shard_map/pallas_call | solution.py:718

commit v5 on v4

--- a/solution.py
+++ b/solution.py
@@ -241,9 +241,11 @@
     d_out.wait_recv()
     gu.g3()
     gd[0].g0()
+    gd[1].g0()
     tok_send(3)
     gu.g4()
-    gd[1].g0()
+    gd[2].g0()
+    gd[3].g0()
     tk["+", 3, 0].wait_recv()
     tk["-", 3, 1].wait_recv()
 
@@ -297,19 +299,19 @@
     norm_half(0)
     gd[0].g1()
     gd[0].g2()
+    gd[1].g1()
+    gd[1].g2()
     norm_half(1)
     gu.g5()
-    gd[2].g0()
-    gd[1].g1()
-    gd[1].g2()
+    gd[2].g1()
+    gd[2].g2()
     gd[0].g3()
     hidden(c)
-    send_act(lambda: c)
+    gd[3].g1()
+    gd[3].g2()
     gd[0].g4()
-    gd[3].g0()
-    gd[2].g1()
-    gd[2].g2()
     gd[1].g3()
+    gd[1].g4()
     for d in n_out:
         d.wait_recv()
 
@@ -576,26 +578,24 @@
                 stage(n, k)
 
     hidden(oc)
-    send_act(lambda: oc)
+    gd[2].g3()
+    gd[2].g4()
     gd[0].g5()
     mixed(0)
-    gd[3].g1()
-    gd[3].g2()
-    gd[1].g4()
-    gd[2].g3()
-    zstage(0, 0)
+    gd[3].g3()
+    gd[3].g4()
     gd[1].g5()
     mixed(1)
-    gd[2].g4()
-    gd[3].g3()
-    zstage(0, 1)
-    zstage(1, 0)
+    zstage(0, 0)
     gd[2].g5()
     mixed(2)
-    gd[3].g4()
+    zstage(1, 0)
+    zstage(0, 1)
     gate_of_student()
     gd[3].g5()
     mixed(3)
+    send_act(lambda: c)
+    send_act(lambda: oc)
     diagonal(2)
     for d in range(3, R + 4):
         diagonal(d)

time: 131 us -> 122 us (0.931)
  Pallas kernels: 128 us -> 119 us
    pallas_call x1, Pallas kernels: 126 us -> 117 us  [shards(): pl.pallas_call(functools.partial(kernel, axes), out_shape=(jax.ShapeDtype...]
where the time goes in v5:
time: 122 us; the launch traced here: 121 us
  Pallas kernels  119 us (98%)
  local copies, waits for them, and re-layouts  1.41 us (1%)
  between operations  1.29 us (1%)
    pallas_call x1, Pallas kernels, shards(): pl.pallas_call(functools.partial(kernel, axes), out_shape=(jax.ShapeDtype...  117 us

profile of v5, /device:TPU:1, one launch (start us, length us, event | category | flops | bytes accessed | tf_op | source)
XLA Modules:
  0.0 121.3 jit_solution(5221801004494466602)
XLA Ops:
  1.3 0.8 constant_dynamic-slice_fusion
  2.1 0.6 copy.11
  2.7 116.6 %shard_map.85 = (bf16[256,384]{1,0:T(8,128)(2,1)}, f32[96,768]{1,0:T(8,128)}, f32[96,768]{1,0:T(8,128)}) custom-call(bf16[256,384]{1,0:T(8,128)(2,1)} %tok_ref.1, bf16[192,768]{1,0:T(8,128)(2,1)} %bitcast.15, bf16[4,48,768]{2,1,0:T(8,128)(2,1)} %bitcast.16, f32[3,3072]{1,0:T(4,128)} %bitcast.17, s32[16]{0:T(128)} %counts_ref.1), custom_call_target="tpu_custom_call" | custom-call | tf_op jit(solution)/shard_map/pallas_call | solution.py:699
  119.2 2.0 %shard_map.86 = (bf16[256,384]{1,0:T(8,128)(2,1)}, f32[96,768]{1,0:T(8,128)}, f32[96,768]{1,0:T(8,128)}) custom-call(bf16[256,384]{1,0:T(8,128)(2,1)} %get-tuple-element.9.out_in, f32[96,768]{1,0:T(8,128)} %get-tuple-element.10.up_in, f32[96,768]{1,0:T(8,128)} %get-tuple-element.11.down_in), custom_call_target="tpu_custom_call" | custom-call | tf_op jit(solution)/shard_map/pallas_call | solution.py:718

commit v6 on v5

--- a/solution.py
+++ b/solution.py
@@ -13,10 +13,22 @@
 ROWS = 192 // R
 RA = (32, 32, 32, 16)
 RU = 112
+ORDER = (
+    ("g2", 3), ("g1", 3), ("hc", 0), ("ho", 0), ("g1", 0), ("g4", 3), ("g2", 0), ("g3", 3), ("g1", 1), ("g2", 1),
+    ("g2", 2), ("g1", 2), ("g3", 0), ("g4", 0), ("g5", 3), ("m", 3), ("g3", 1), ("g4", 1), ("g4", 2), ("s0", 3),
+    ("g3", 2), ("g5", 0), ("m", 0), ("g5", 1), ("m", 1), ("s1", 3), ("g5", 2), ("m", 2), ("s0", 0), ("s0", 1),
+    ("s0", 2), ("s2", 3), ("s1", 0), ("s1", 1), ("s1", 2), ("s3", 3), ("s2", 0), ("s2", 1), ("s2", 2), ("s4", 3),
+    ("s3", 0), ("s3", 1), ("s3", 2), ("s4", 0), ("s5", 3), ("s4", 1), ("s4", 2), ("s6", 3), ("s5", 0), ("s5", 1),
+    ("s5", 2), ("s7", 3), ("s6", 0), ("s6", 1), ("s6", 2), ("s8", 3), ("s7", 0), ("s7", 1), ("s7", 2), ("s9", 3),
+    ("s8", 0), ("s10", 3), ("s8", 1), ("s8", 2), ("s9", 0), ("s9", 1), ("s10", 0), ("s9", 2), ("s10", 1), ("s10", 2),
+    ("b", 1), ("b", 0), ("b", 3), ("b", 2), ("r1", 1), ("r2", 1), ("r1", 0), ("r1", 3), ("r1", 2), ("r2", 0),
+    ("r4", 1), ("r3", 1), ("r4", 0), ("r2", 3), ("r4", 3), ("r2", 2), ("r4", 2), ("r3", 0), ("r5", 1), ("r3", 3),
+    ("r3", 2), ("r6", 1), ("r5", 0), ("r6", 0), ("r5", 3), ("r5", 2), ("r6", 3), ("r7", 1), ("r6", 2), ("r7", 0),
+)
 NZ = 8
 SEQ = 256
 BLK = 384
-N_RECV = 145
+N_RECV = 161
 N_SEND = {None: 40, 1: 2}
 
 
@@ -44,9 +56,9 @@
 
 def kernel(
     axes,
-    tok_ref, up_ref, downt_ref, mod_ref, counts_ref,
+    tok_ref, up_ref, downt_ref, table_ref, step_ref, counts_ref,
     out_ref, ug_ref, dg_ref,
-    T, U, D, N, NTR, HP, SL, ACT, ACTG, PO, PS, PR, ZS, ZR, MODO, GATE, GATEG, TOKT, OTA, OTB, GT, GA, GP,
+    T, ST, MEAN, RSTD, U, D, N, NTR, HP, SL, ACT, ACTG, PO, PS, PR, ZS, ZR, TAB, mod_ref, MODO, GATE, GATEG, TOKT, OTA, OTB, GT, GA, GP,
     QV, XBS, XBR, A2S, A2R, A1S, A1R, B2S, B2R, B1S, B1R, AXS, AXR, FS, FO, FR, HS, HR,
     send, recv, local,
 ):
@@ -76,6 +88,8 @@
     C = where(dp_=dp + 1 - 2 * c)
     S = where(side_=1 - s)
 
+    table_in = pltpu.make_async_copy(table_ref, TAB, local.at[3])
+    table_in.start()
     barrier = pltpu.get_barrier_semaphore()
     peers = (X, YP, YM, ZP, ZM, C, S)
     for peer in peers:
@@ -150,11 +164,13 @@
 
         def g2(self):
             self.yp.wait_recv()
-            self.rp = copy_same(lambda: self.buf(jj(xl, ym)).at[0], YP)
+            self.rp = copy_same(lambda: self.bpart(xl, ym).at[0], YP)
             self.bxm = copy_same(lambda: self.bpart(xl, ym), X, at=self.bx)
+            self.rpa = copy_same(lambda: self.apart(xl, ym).at[0], YP)
             self.ym.wait_recv()
-            self.rm = copy_same(lambda: self.buf(jj(xl, yp)).at[1], YM)
+            self.rm = copy_same(lambda: self.bpart(xl, yp).at[1], YM)
             self.bxp = copy_same(lambda: self.bpart(xl, yp), X, at=self.bx)
+            self.rma = copy_same(lambda: self.apart(xl, yp).at[1], YM)
 
         def g3(self):
             self.xap.wait_recv()
@@ -168,8 +184,8 @@
             self.bx2 = copy_same(lambda: self.bpart(xl, y2), X, at=self.bx)
 
         def g5(self):
-            self.rxp.wait_recv()
-            self.rxm.wait_recv()
+            for d in (self.rpa, self.rma, self.rxp, self.rxm):
+                d.wait_recv()
             wait_bytes(self.bx, self.four())
 
     own = jj(xl, y)
@@ -186,22 +202,65 @@
 
     tk = {}
 
-    def tok_send(hop):
-        for p in range(2):
-            rows = pl.ds(128 * p, 128)
-            if hop:
-                if ("+", hop - 1, p) in tk:
-                    tk["+", hop - 1, p].wait_recv()
-            at = functools.partial(lambda k, rows: tok_ref.at[rows] if k is None else T.at[zz(k), rows], rows=rows)
-            src = functools.partial(at, None if hop == 0 else -hop)
-            if hop < 3 or p == 0:
-                tk["+", hop, p] = copy(src, functools.partial(at, -hop), ZP)
-            if hop:
-                if ("-", hop - 1, p) in tk:
-                    tk["-", hop - 1, p].wait_recv()
-            src = functools.partial(at, None if hop == 0 else hop)
-            if hop < 3 or p == 1:
-                tk["-", hop, p] = copy(src, functools.partial(at, hop), ZM)
+    def tok(hop, p):
+        rows = pl.ds(128 * p, 128)
+        for q, sign, dev in ((0, -1, ZP), (1, 1, ZM)):
+            if (q, hop - 1, p) in tk:
+                tk[q, hop - 1, p].wait_recv()
+            if hop < 3 or hop == 3 and p == q:
+                at = functools.partial(lambda k, rows: tok_ref.at[rows] if k is None else T.at[zz(k), rows], rows=rows)
+                src = functools.partial(at, None if hop == 0 else sign * hop)
+                tk[q, hop, p] = copy(src, functools.partial(at, sign * hop), dev)
+
+    st = {}
+
+    def stats(hop):
+        for q, sign, dev in ((0, -1, ZP), (1, 1, ZM)):
+            if (q, hop - 1) in st:
+                st[q, hop - 1].wait_recv()
+            if hop < 3 or hop == 3 and q == 0:
+                st[q, hop] = copy_same(functools.partial(lambda k: ST.at[zz(k)], sign * hop), dev)
+
+    def own_stats():
+        x = T[z].astype(F32)
+        m = jnp.sum(x, axis=-1, keepdims=True) * (1.0 / BLK)
+        x = x - m
+        sq = jnp.sum(x * x, axis=-1, keepdims=True)
+        lane = lax.broadcasted_iota(jnp.int32, (SEQ, 128), 1)
+        ST[z] = jnp.transpose(jnp.where(lane == 0, m, sq))[0:8]
+
+    def all_stats():
+        ms = [ST[b, 0:1] for b in range(NZ)]
+        mean = ms[0]
+        sq = ST[0, 1:2]
+        for b in range(1, NZ):
+            mean = mean + ms[b]
+            sq = sq + ST[b, 1:2]
+        mean = mean * (1.0 / NZ)
+        apart = (ms[0] - mean) * (ms[0] - mean)
+        for b in range(1, NZ):
+            apart = apart + (ms[b] - mean) * (ms[b] - mean)
+        rs = lax.rsqrt((sq + BLK * apart) * (1.0 / (NZ * BLK)) + 1e-06)
+        MEAN[...] = jnp.transpose(jnp.broadcast_to(mean, (128, SEQ)))
+        RSTD[...] = jnp.transpose(jnp.broadcast_to(rs, (128, SEQ)))
+
+    n_sem = used[0]
+    used[0] += 1
+
+    def norm(k, p):
+        b = zz(k)
+        at = pl.ds(pl.multiple_of(b * BLK, 128), BLK)
+        scale, shift = 1.0 + mod_ref[1:2, at], mod_ref[0:1, at]
+
+        def tile(i, carry):
+            rows = pl.ds(pl.multiple_of(128 * p + i * 32, 32), 32)
+            m, rs = MEAN[rows], RSTD[rows]
+            m, rs = jnp.concatenate([m] * 3, axis=1), jnp.concatenate([rs] * 3, axis=1)
+            N[c, b, rows] = ((T[b, rows].astype(F32) - m) * rs * scale + shift).astype(BF)
+            return carry
+
+        lax.fori_loop(0, 4, tile, 0)
+        copy_same(lambda: N.at[c, zz(k), pl.ds(128 * p, 128)], C, at=n_sem)
 
     gu = Gather(lambda j: U.at[j], RU, lambda: U.at[0:4, :, RU:192])
     gd = [
@@ -212,12 +271,21 @@
         for r in range(R)
     ]
 
-    tok_send(0)
-    mod_out = copy(lambda: mod_ref, lambda: MODO, S)
+    tok(0, 0)
     u_in.wait()
     u_out.wait_recv()
     gu.g0()
     tok_in.wait()
+    own_stats()
+    stats(0)
+    tok(0, 1)
+    table_in.wait()
+    n = 3 * NZ * BLK // 128
+    plan = TAB[step_ref[0]]
+    for i in range(n):
+        k, at = divmod(128 * i, NZ * BLK)
+        mod_ref[k:k + 1, at:at + 128] = plan[i:i + 1]
+    mod_out = copy(lambda: mod_ref, lambda: MODO, S)
     gate = mod_ref[2:3, pl.ds(pl.multiple_of(z * BLK, 128), BLK)]
     gate = jnp.transpose(jnp.broadcast_to(gate, (128, BLK)))
     GATE[:, 0:128] = gate
@@ -233,46 +301,41 @@
 
     tt = jnp.transpose(T[z].astype(F32))
     TOKT[...] = tt
-    tok_send(1)
+    stats(1)
+    tok(1, 0)
     gu.g1()
-    tok_send(2)
+    tok(1, 1)
+    stats(2)
     gu.g2()
+    tok(2, 0)
+    stats(3)
+    tok(2, 1)
     d_in.wait()
     d_out.wait_recv()
     gu.g3()
+    gd[3].g0()
+    st[0, 3].wait_recv()
+    all_stats()
+    for k in (0, -1, 1):
+        for p in range(2):
+            norm(k, p)
+    gu.g4()
+    gd[1].g0()
+    tok(3, 0)
+    norm(-2, 0)
+    norm(2, 0)
+    tok(3, 1)
+    norm(-2, 1)
+    norm(2, 1)
     gd[0].g0()
-    gd[1].g0()
-    tok_send(3)
-    gu.g4()
+    for k in (-3, 3):
+        for p in range(2):
+            norm(k, p)
+    tok(4, 0)
+    norm(4, 0)
+    tok(4, 1)
+    norm(4, 1)
     gd[2].g0()
-    gd[3].g0()
-    tk["+", 3, 0].wait_recv()
-    tk["-", 3, 1].wait_recv()
-
-    def norm_rows(i, carry):
-        rows = pl.ds(pl.multiple_of(i * 16, 16), 16)
-        x = [T[b, rows].astype(F32) for b in range(NZ)]
-        total = x[0]
-        for b in range(1, NZ):
-            total = total + x[b]
-        mean = jnp.sum(total, axis=-1, keepdims=True) * (1.0 / (NZ * BLK))
-        x = [v - mean for v in x]
-        sq = x[0] * x[0]
-        for b in range(1, NZ):
-            sq = sq + x[b] * x[b]
-        var = jnp.sum(sq, axis=-1, keepdims=True) * (1.0 / (NZ * BLK))
-        rs = lax.rsqrt(var + 1e-06)
-        for b in range(NZ):
-            cols = slice(b * BLK, (b + 1) * BLK)
-            n = x[b] * rs * (1.0 + mod_ref[1:2, cols]) + mod_ref[0:1, cols]
-            N[c, b, rows] = n.astype(BF)
-        return carry
-
-    n_out = []
-
-    def norm_half(p):
-        lax.fori_loop(8 * p, 8 * p + 8, norm_rows, 0)
-        n_out.append(copy_same(lambda: N.at[c, :, pl.ds(128 * p, 128)], C))
 
     def hidden(img):
         h = nn(N[img, 0], U[0].reshape(BLK, BLK))
@@ -295,25 +358,6 @@
         @pl.when(student)
         def _():
             act_out.append(copy(lambda: ACT.at[img()], lambda: ACTG.at[img()], S, 1))
-
-    norm_half(0)
-    gd[0].g1()
-    gd[0].g2()
-    gd[1].g1()
-    gd[1].g2()
-    norm_half(1)
-    gu.g5()
-    gd[2].g1()
-    gd[2].g2()
-    gd[0].g3()
-    hidden(c)
-    gd[3].g1()
-    gd[3].g2()
-    gd[0].g4()
-    gd[1].g3()
-    gd[1].g4()
-    for d in n_out:
-        d.wait_recv()
 
     m_out, zs = {}, {}
     z_sems = used[0]
@@ -523,11 +567,11 @@
         q = nn(g[0], ACTG[0]) + nn(g[1], ACTG[1])
         QV[r] = q.reshape(NZ, 2, ROWS, BLK)
 
-    def grad_act(r):
+    def grad_act(r, first):
         w = D[r].reshape(NZ * 2 * ROWS, BLK)
         for img in range(2):
             v = tn(GT[r, img], w)
-            if r == 0:
+            if first:
                 GA[img] = v
             else:
                 GA[img] += v
@@ -547,11 +591,10 @@
         lax.fori_loop(4 * part, 4 * part + 4, one, 0)
 
     def up_grads(r):
-        if r == 0:
-            for img in range(2):
-                GP[img] = (GA[img] * SL[img]).astype(BF)
         q = nn(NTR[r, 0], GP[0]) + nn(NTR[r, 1], GP[1])
         QV[r] = q.reshape(NZ, 2, ROWS, BLK)
+
+    summed = []
 
     def stage(n, k):
         if k < 4:
@@ -562,76 +605,60 @@
             astage(n, k - 5)
         else:
             arrived(n)
-            pl.when(student)(lambda: grad_act(n))
+            first = not summed
+            summed.append(n)
+            pl.when(student)(lambda: grad_act(n, first))
 
             @pl.when(s == 0)
             def _():
-                if n == 0:
+                if first:
                     for d in act_out:
                         d.wait_recv()
                 down_grads(n)
 
-    def diagonal(d):
-        for n in reversed(range(R)):
-            k = d - n
-            if 0 <= k < 11:
-                stage(n, k)
-
-    hidden(oc)
-    gd[2].g3()
-    gd[2].g4()
-    gd[0].g5()
-    mixed(0)
-    gd[3].g3()
-    gd[3].g4()
-    gd[1].g5()
-    mixed(1)
-    zstage(0, 0)
-    gd[2].g5()
-    mixed(2)
-    zstage(1, 0)
-    zstage(0, 1)
-    gate_of_student()
-    gd[3].g5()
-    mixed(3)
-    send_act(lambda: c)
-    send_act(lambda: oc)
-    diagonal(2)
-    for d in range(3, R + 4):
-        diagonal(d)
-    out_ref[...] = jnp.transpose(TOKT[...]).astype(BF)
-    for d in range(R + 4, 11 + R - 1):
-        diagonal(d)
-        if d < R + 8:
-            pl.when(student)(lambda: transposed(d - R - 4))
-
     def begin(n):
+        if not begun:
+            out_ref[...] = jnp.transpose(TOKT[...]).astype(BF)
+
+            @pl.when(student)
+            def _():
+                for img in range(2):
+                    GP[img] = (GA[img] * SL[img]).astype(BF)
+
+        begun.append(n)
         pl.when(student)(lambda: up_grads(n))
         red[n].r0()
 
-    def rstage(n, k):
-        if k == 0:
+    begun, mixed_of, swapped, far = [], [], [], []
+    gu.g5()
+    for what, n in ORDER:
+        if what == "hc":
+            hidden(c)
+        elif what == "ho":
+            wait_bytes(n_sem, N.at[oc])
+            hidden(oc)
+        elif what[0] == "g":
+            getattr(gd[n], what)()
+        elif what == "m":
+            mixed(n)
+            mixed_of.append(n)
+            if len(mixed_of) == R:
+                send_act(lambda: c)
+                send_act(lambda: oc)
+        elif what[0] == "s":
+            k = int(what[1:])
+            if k == 5:
+                if not swapped:
+                    gate_of_student()
+                swapped.append(n)
+            stage(n, k)
+            if k == 8:
+                pl.when(student)(functools.partial(transposed, len(far)))
+                far.append(n)
+        elif what == "b":
             begin(n)
-        elif k == 1:
-            red[n].r1()
-            red[n].r2()
-        elif k == 2:
-            red[n].r3()
-            red[n].r4()
-        elif k == 3:
-            red[n].r5()
         else:
-            red[n].r6()
-
-    begin(0)
-    begin(1)
-    for d in range(2, R + 5):
-        for n in reversed(range(R)):
-            k = d - n if d - n < 1 else d - n - 1
-            if d - n == 0 and n > 1 or 1 <= k < 5 and d - n > 1:
-                rstage(n, k)
-    for n in range(R // 2):
-        red[n].r7()
+            getattr(red[n], what)()
 
     for d in started[None][-N_SEND[None]:]:
         d.wait_send()
@@ -643,13 +670,16 @@
 
 
 def shards(axes, tokens, up_weight, down_weight, mod_table, timesteps, valid_counts):
-    mod = lax.dynamic_index_in_dim(mod_table[0], timesteps[0], 0, keepdims=False)
+    table = mod_table.reshape(mod_table.shape[1], -1, 128)
     downt = down_weight[0].T.reshape(R, ROWS, 2 * BLK)
 
     v = pltpu.VMEM
     nred = R
     scratch = [
         v((NZ, SEQ, BLK), BF),
+        v((NZ, 8, SEQ), F32),
+        v((SEQ, 128), F32),
+        v((SEQ, 128), F32),
         v((NZ, 2, 192, BLK), BF),
         v((R, NZ, 2, ROWS, BLK), BF),
         v((2, NZ, SEQ, BLK), BF),
@@ -663,6 +693,8 @@
         v((R, NZ * 2 * ROWS, SEQ), BF),
         v((R, 2, 4, 2 * ROWS, SEQ), BF),
         v((R, 2, 4, 2 * ROWS, SEQ), BF),
+        v(table.shape, F32),
+        v((3, NZ * BLK), F32),
         v((3, NZ * BLK), F32),
         v((BLK, SEQ), F32),
         v((BLK, SEQ), F32),
@@ -692,7 +724,7 @@
         v((nred, 2, ROWS, BLK), BF),
         pltpu.SemaphoreType.DMA((sum(N_SEND.values()),)),
         pltpu.SemaphoreType.DMA((N_RECV,)),
-        pltpu.SemaphoreType.DMA((3,)),
+        pltpu.SemaphoreType.DMA((4,)),
     ]
     hbm = pl.BlockSpec(memory_space=pl.ANY)
     vm = pl.BlockSpec(memory_space=pltpu.VMEM)
@@ -703,13 +735,13 @@
             jax.ShapeDtypeStruct((96, 2 * BLK), F32),
             jax.ShapeDtypeStruct((96, 2 * BLK), F32),
         ),
-        in_specs=[hbm, hbm, hbm, vm, pl.BlockSpec(memory_space=pltpu.SMEM)],
+        in_specs=[hbm, hbm, hbm, hbm] + [pl.BlockSpec(memory_space=pltpu.SMEM)] * 2,
         out_specs=(vm, vm, vm),
         scratch_shapes=scratch,
         compiler_params=pltpu.CompilerParams(
             collective_id=0, has_side_effects=True, vmem_limit_bytes=67043328
         ),
-    )(tokens, up_weight[0], downt, mod, valid_counts)
+    )(tokens, up_weight[0], downt, table, timesteps, valid_counts)
     def settle(out_in, up_in, down_in, out_to, up_to, down_to):
         out_to[...] = out_in[...]
         up_to[...] = up_in[...]

time: 122 us -> 119 us (0.975)
  Pallas kernels: 119 us -> 117 us
  local copies, waits for them, and re-layouts: 1.41 us -> 0 us
    pallas_call x1, Pallas kernels: 117 us -> 115 us  [shards(): pl.pallas_call(functools.partial(kernel, axes), out_shape=(jax.ShapeDtype...]
where the time goes in v6:
time: 119 us
  Pallas kernels  117 us (98%)
  between operations  1.29 us (1%)
    pallas_call x1, Pallas kernels, shards(): pl.pallas_call(functools.partial(kernel, axes), out_shape=(jax.ShapeDtype...  115 us

profile of v6, /device:TPU:1, one launch (start us, length us, event | category | flops | bytes accessed | tf_op | source)
XLA Modules:
  0.0 118.7 jit_solution(3326830678062637199)
XLA Ops:
  1.3 115.3 %shard_map.85 = (bf16[256,384]{1,0:T(8,128)(2,1)}, f32[96,768]{1,0:T(8,128)}, f32[96,768]{1,0:T(8,128)}) custom-call(bf16[256,384]{1,0:T(8,128)(2,1)} %tok_ref.1, bf16[192,768]{1,0:T(8,128)(2,1)} %bitcast.10, bf16[4,48,768]{2,1,0:T(8,128)(2,1)} %bitcast.11, f32[50,72,128]{2,1,0:T(8,128)} %bitcast.9, s32[1]{0:T(128)S(6)} %copy.9.step_ref, s32[16]{0:T(128)} %counts_ref.1), custom_call_target="tpu_custom_call" | custom-call | tf_op jit(solution)/shard_map/pallas_call | solution.py:731
  116.6 2.0 %shard_map.86 = (bf16[256,384]{1,0:T(8,128)(2,1)}, f32[96,768]{1,0:T(8,128)}, f32[96,768]{1,0:T(8,128)}) custom-call(bf16[256,384]{1,0:T(8,128)(2,1)} %get-tuple-element.9.out_in, f32[96,768]{1,0:T(8,128)} %get-tuple-element.10.up_in, f32[96,768]{1,0:T(8,128)} %get-tuple-element.11.down_in), custom_call_target="tpu_custom_call" | custom-call | tf_op jit(solution)/shard_map/pallas_call | solution.py:750

commit v7 on v6

--- a/solution.py
+++ b/solution.py
@@ -28,18 +28,21 @@
 NZ = 8
 SEQ = 256
 BLK = 384
-N_RECV = 161
+N_RECV = 121
 N_SEND = {None: 40, 1: 2}
 
 
-def gelu_pair(v):
-    k = 0.7978845608028654
+K = 0.7978845608028654
+
+
+def gelu(v):
+    return v * (0.5 * (1.0 + jnp.tanh(K * v * (1.0 + 0.044715 * (v * v)))))
+
+
+def gelu_slope(v):
     v2 = v * v
-    t = jnp.tanh(k * v * (1.0 + 0.044715 * v2))
-    half = 0.5 * (1.0 + t)
-    act = v * half
-    slope = half + 0.5 * v * (1.0 - t * t) * (k * (1.0 + 3.0 * 0.044715 * v2))
-    return act, slope
+    t = jnp.tanh(K * v * (1.0 + 0.044715 * v2))
+    return 0.5 * (1.0 + t) + 0.5 * v * (1.0 - t * t) * (K * (1.0 + 3.0 * 0.044715 * v2))
 
 
 def nn(a, b):
@@ -56,9 +59,9 @@
 
 def kernel(
     axes,
-    tok_ref, up_ref, downt_ref, table_ref, step_ref, counts_ref,
+    tok_ref, up_ref, downt_ref, table_ref, step_in, counts_in,
     out_ref, ug_ref, dg_ref,
-    T, ST, MEAN, RSTD, U, D, N, NTR, HP, SL, ACT, ACTG, PO, PS, PR, ZS, ZR, TAB, mod_ref, MODO, GATE, GATEG, TOKT, OTA, OTB, GT, GA, GP,
+    T, ST, MEAN, RSTD, U, D, N, NTR, HP, SL, ACT, ACTG, PO, PS, PR, ZS, ZR, TAB, step_ref, counts_ref, mod_ref, MODO, GATE, GATEG, TOKT, OTA, OTB, GT, GA, GP,
     QV, XBS, XBR, A2S, A2R, A1S, A1R, B2S, B2R, B1S, B1R, AXS, AXR, FS, FO, FR, HS, HR,
     send, recv, local,
 ):
@@ -90,6 +93,10 @@
 
     table_in = pltpu.make_async_copy(table_ref, TAB, local.at[3])
     table_in.start()
+    step_copy = pltpu.make_async_copy(step_in, step_ref, local.at[4])
+    step_copy.start()
+    counts_copy = pltpu.make_async_copy(counts_in, counts_ref, local.at[5])
+    counts_copy.start()
     barrier = pltpu.get_barrier_semaphore()
     peers = (X, YP, YM, ZP, ZM, C, S)
     for peer in peers:
@@ -138,9 +145,13 @@
 
     student = s == 1
 
+    class Whole:
+        def __init__(self, i, ref):
+            self.wait_recv = lambda: wait_bytes(i, ref())
+
     class Gather:
-        def __init__(self, buf, ra, four):
-            self.buf, self.ra, self.four = buf, ra, four
+        def __init__(self, buf, ra, two, four):
+            self.buf, self.ra, self.two, self.four = buf, ra, two, four
 
         def g0(self):
             self.bx = used[0]
@@ -150,6 +161,27 @@
             self.ym = copy_same(lambda: self.buf(own), YM)
             self.xb = copy_same(lambda: self.bpart(xl, y), X, at=self.bx)
 
+        def direct(self, mine):
+            if mine:
+                self.xi, self.yi, self.wi, self.bx = range(used[0], used[0] + 4)
+                used[0] += 4
+            h, ra = (c if mine else oc), self.ra
+            cols = pl.ds(pl.multiple_of(c * BLK, 128), BLK)
+
+            def send(dev, rows, at):
+                copy(
+                    lambda: up_ref.at[rows, cols] if mine else self.buf(own).at[h, rows],
+                    lambda: self.buf(own).at[h, rows], dev, None, at,
+                )
+
+            send(X, pl.ds(0, ra), self.xi)
+            send(YP, pl.ds(0, 192), self.yi)
+            send(YM, pl.ds(0, 192), self.wi)
+            send(X, pl.ds(ra, 192 - ra), self.bx)
+            self.xa = Whole(self.xi, lambda: self.apart(xo, y))
+            self.yp = Whole(self.yi, lambda: self.buf(jj(xl, ym)))
+            self.ym = Whole(self.wi, lambda: self.buf(jj(xl, yp)))
+
         def g1(self):
             self.xa.wait_recv()
             self.xap = copy_same(lambda: self.apart(xo, y), YP)
@@ -164,19 +196,21 @@
 
         def g2(self):
             self.yp.wait_recv()
+            late = self.late = used[0]
+            used[0] += 1
             self.rp = copy_same(lambda: self.bpart(xl, ym).at[0], YP)
             self.bxm = copy_same(lambda: self.bpart(xl, ym), X, at=self.bx)
-            self.rpa = copy_same(lambda: self.apart(xl, ym).at[0], YP)
+            copy_same(lambda: self.apart(xl, ym).at[0], YP, None, late)
             self.ym.wait_recv()
             self.rm = copy_same(lambda: self.bpart(xl, yp).at[1], YM)
             self.bxp = copy_same(lambda: self.bpart(xl, yp), X, at=self.bx)
-            self.rma = copy_same(lambda: self.apart(xl, yp).at[1], YM)
+            copy_same(lambda: self.apart(xl, yp).at[1], YM, None, late)
 
         def g3(self):
             self.xap.wait_recv()
-            self.rxp = copy_same(lambda: self.buf(jj(xo, ym)).at[0, pl.ds(0, self.ra)], YP)
+            copy_same(lambda: self.buf(jj(xo, ym)).at[0, pl.ds(0, self.ra)], YP, None, self.late)
             self.xam.wait_recv()
-            self.rxm = copy_same(lambda: self.buf(jj(xo, yp)).at[1, pl.ds(0, self.ra)], YM)
+            copy_same(lambda: self.buf(jj(xo, yp)).at[1, pl.ds(0, self.ra)], YM, None, self.late)
 
         def g4(self):
             self.rp.wait_recv()
@@ -184,13 +218,13 @@
             self.bx2 = copy_same(lambda: self.bpart(xl, y2), X, at=self.bx)
 
         def g5(self):
-            for d in (self.rpa, self.rma, self.rxp, self.rxm):
-                d.wait_recv()
+            wait_bytes(self.late, self.two())
             wait_bytes(self.bx, self.four())
 
     own = jj(xl, y)
     u_out = copy(lambda: up_ref.at[:, pl.ds(pl.multiple_of(oc * BLK, 128), BLK)], lambda: U.at[own, c], C)
-    d_out = copy(lambda: downt_ref.at[:, :, pl.ds(pl.multiple_of(oc * BLK, 128), BLK)], lambda: D.at[:, own, c], C)
+    gu = Gather(lambda j: U.at[j], RU, lambda: U.at[0:2, :, 0:RU], lambda: U.at[0:4, :, RU:192])
+    gu.direct(True)
     tok_in = pltpu.make_async_copy(tok_ref, T.at[z], local.at[0])
     tok_in.start()
     u_in = pltpu.make_async_copy(up_ref.at[:, pl.ds(pl.multiple_of(c * BLK, 128), BLK)], U.at[own, c], local.at[1])
@@ -201,25 +235,31 @@
     d_in.start()
 
     tk = {}
+    t_sems = used[0]
+    used[0] += 12
 
     def tok(hop, p):
         rows = pl.ds(128 * p, 128)
-        for q, sign, dev in ((0, -1, ZP), (1, 1, ZM)):
+        for q in range(2):
             if (q, hop - 1, p) in tk:
                 tk[q, hop - 1, p].wait_recv()
+        for q, sign, dev in ((0, -1, ZP), (1, 1, ZM)):
             if hop < 3 or hop == 3 and p == q:
                 at = functools.partial(lambda k, rows: tok_ref.at[rows] if k is None else T.at[zz(k), rows], rows=rows)
                 src = functools.partial(at, None if hop == 0 else sign * hop)
-                tk[q, hop, p] = copy(src, functools.partial(at, sign * hop), dev)
+                tk[q, hop, p] = copy(src, functools.partial(at, sign * hop), dev, None, t_sems + 4 * p + 2 * q + hop % 2)
 
     st = {}
 
     def stats(hop):
-        for q, sign, dev in ((0, -1, ZP), (1, 1, ZM)):
+        for q in range(2):
             if (q, hop - 1) in st:
                 st[q, hop - 1].wait_recv()
+        for q, sign, dev in ((0, -1, ZP), (1, 1, ZM)):
             if hop < 3 or hop == 3 and q == 0:
-                st[q, hop] = copy_same(functools.partial(lambda k: ST.at[zz(k)], sign * hop), dev)
+                st[q, hop] = copy_same(
+                    functools.partial(lambda k: ST.at[zz(k)], sign * hop), dev, None, t_sems + 8 + 2 * q + hop % 2
+                )
 
     def own_stats():
         x = T[z].astype(F32)
@@ -262,24 +302,26 @@
         lax.fori_loop(0, 4, tile, 0)
         copy_same(lambda: N.at[c, zz(k), pl.ds(128 * p, 128)], C, at=n_sem)
 
-    gu = Gather(lambda j: U.at[j], RU, lambda: U.at[0:4, :, RU:192])
     gd = [
         Gather(
             functools.partial(lambda r, j: D.at[r, j], r), RA[r],
+            functools.partial(lambda r: D.at[r, 0:2, :, 0:RA[r]], r),
             functools.partial(lambda r: D.at[r, 0:4, :, RA[r]:ROWS], r),
         )
         for r in range(R)
     ]
 
     tok(0, 0)
-    u_in.wait()
     u_out.wait_recv()
-    gu.g0()
+    gu.direct(False)
     tok_in.wait()
     own_stats()
     stats(0)
     tok(0, 1)
+    d_out = copy(lambda: downt_ref.at[:, :, pl.ds(pl.multiple_of(oc * BLK, 128), BLK)], lambda: D.at[:, own, c], C)
     table_in.wait()
+    step_copy.wait()
+    counts_copy.wait()
     n = 3 * NZ * BLK // 128
     plan = TAB[step_ref[0]]
     for i in range(n):
@@ -341,16 +383,22 @@
         h = nn(N[img, 0], U[0].reshape(BLK, BLK))
         for b in range(1, NZ):
             h = h + nn(N[img, b], U[b].reshape(BLK, BLK))
-        HP[...] = h
+        HP[img] = h
 
         def act_rows(i, carry):
             rows = pl.ds(pl.multiple_of(i * 32, 32), 32)
-            a, g = gelu_pair(HP[rows])
-            ACT[img, rows] = a.astype(BF)
-            SL[img, rows] = g
+            ACT[img, rows] = gelu(HP[img, rows]).astype(BF)
             return carry
 
         lax.fori_loop(0, SEQ // 32, act_rows, 0)
+
+    def slopes(img):
+        def rows_of_slope(i, carry):
+            rows = pl.ds(pl.multiple_of(i * 32, 32), 32)
+            SL[img, rows] = gelu_slope(HP[img, rows])
+            return carry
+
+        lax.fori_loop(0, SEQ // 32, rows_of_slope, 0)
 
     act_out = []
 
@@ -464,10 +512,11 @@
             self.r = lax.rem(i + 2 * (1 - s), R)
 
         def both(self, src, dst):
-            def one(h):
-                return copy(lambda: src().at[h], lambda: dst().at[h], (YP, YM)[h])
-
-            return [one(0), one(1)]
+            at = used[0]
+            used[0] += 1
+            for h in range(2):
+                copy(lambda: src().at[h], lambda: dst().at[h], (YP, YM)[h], None, at)
+            return Whole(at, dst)
 
         def q(self, j, rows):
             return QV[self.r, j, :, rows]
@@ -484,8 +533,8 @@
 
         def r1(self):
             i, ra = self.i, self.ra
+            self.a2.wait_recv()
             for h in range(2):
-                self.a2[h].wait_recv()
                 for x in range(2):
                     v = self.q(jj(x, (yp, ym)[h]), self.a)
                     A1S[i, h, x, h, ra] = (v[h] + A2R[i, h, x, ra].astype(F32)).astype(BF)
@@ -501,8 +550,8 @@
 
         def r3(self):
             i, rb = self.i, self.rb
+            self.b2.wait_recv()
             for h in range(2):
-                self.b2[h].wait_recv()
                 yy = (yp, ym)[h]
                 v = self.q(jj(xl, yy), self.b) + XBR[i, yy, :, rb].astype(F32)
                 B1S[i, h, h, rb] = (v[h] + B2R[i, h, rb].astype(F32)).astype(BF)
@@ -511,8 +560,7 @@
 
         def r4(self):
             i, ra = self.i, self.ra
-            for h in range(2):
-                self.a1[h].wait_recv()
+            self.a1.wait_recv()
             v = self.q(jj(xo, y), self.a) + A1R[i, 0, xo, :, ra].astype(F32) + A1R[i, 1, xo, :, ra].astype(F32)
             AXS[i, :, ra] = v.astype(BF)
             self.ax = copy(lambda: AXS.at[i, :, ra], lambda: AXR.at[i, :, ra], X)
@@ -521,8 +569,7 @@
             i, ra, rb = self.i, self.ra, self.rb
             va = self.q(own, self.a) + A1R[i, 0, xl, :, ra].astype(F32) + A1R[i, 1, xl, :, ra].astype(F32)
             vb = self.q(own, self.b) + XBR[i, y, :, rb].astype(F32)
-            for d in self.b1:
-                d.wait_recv()
+            self.b1.wait_recv()
             vb = vb + B1R[i, 0, :, rb].astype(F32) + B1R[i, 1, :, rb].astype(F32)
             self.ax.wait_recv()
             FO[i, :, self.a] = va + AXR[i, :, ra].astype(F32)
@@ -618,8 +665,6 @@
 
     def begin(n):
         if not begun:
-            out_ref[...] = jnp.transpose(TOKT[...]).astype(BF)
-
             @pl.when(student)
             def _():
                 for img in range(2):
@@ -629,7 +674,8 @@
         pl.when(student)(lambda: up_grads(n))
         red[n].r0()
 
-    begun, mixed_of, swapped, far = [], [], [], []
+    u_in.wait()
+    begun, mixed_of, swapped, far, put, sloped = [], [], [], [], [], []
     gu.g5()
     for what, n in ORDER:
         if what == "hc":
@@ -652,6 +698,13 @@
                     gate_of_student()
                 swapped.append(n)
             stage(n, k)
+            if k == 4:
+                put.append(n)
+                if len(put) == R:
+                    out_ref[...] = jnp.transpose(TOKT[...]).astype(BF)
+            if k == 6 and len(sloped) < 2:
+                pl.when(student)(functools.partial(slopes, len(sloped)))
+                sloped.append(n)
             if k == 8:
                 pl.when(student)(functools.partial(transposed, len(far)))
                 far.append(n)
@@ -684,7 +737,7 @@
         v((R, NZ, 2, ROWS, BLK), BF),
         v((2, NZ, SEQ, BLK), BF),
         v((R, 2, NZ * 2 * ROWS, SEQ), BF),
-        v((SEQ, BLK), F32),
+        v((2, SEQ, BLK), F32),
         v((2, SEQ, BLK), F32),
         v((2, SEQ, BLK), BF),
         v((2, SEQ, BLK), BF),
@@ -694,6 +747,8 @@
         v((R, 2, 4, 2 * ROWS, SEQ), BF),
         v((R, 2, 4, 2 * ROWS, SEQ), BF),
         v(table.shape, F32),
+        pltpu.SMEM(timesteps.shape, jnp.int32),
+        pltpu.SMEM(valid_counts.shape, jnp.int32),
         v((3, NZ * BLK), F32),
         v((3, NZ * BLK), F32),
         v((BLK, SEQ), F32),
@@ -724,7 +779,7 @@
         v((nred, 2, ROWS, BLK), BF),
         pltpu.SemaphoreType.DMA((sum(N_SEND.values()),)),
         pltpu.SemaphoreType.DMA((N_RECV,)),
-        pltpu.SemaphoreType.DMA((4,)),
+        pltpu.SemaphoreType.DMA((6,)),
     ]
     hbm = pl.BlockSpec(memory_space=pl.ANY)
     vm = pl.BlockSpec(memory_space=pltpu.VMEM)
@@ -735,7 +790,7 @@
             jax.ShapeDtypeStruct((96, 2 * BLK), F32),
             jax.ShapeDtypeStruct((96, 2 * BLK), F32),
         ),
-        in_specs=[hbm, hbm, hbm, hbm] + [pl.BlockSpec(memory_space=pltpu.SMEM)] * 2,
+        in_specs=[hbm] * 6,
         out_specs=(vm, vm, vm),
         scratch_shapes=scratch,
         compiler_params=pltpu.CompilerParams(

time: 119 us -> 118 us (level)
  no operation moved by 1% of the time
where the time goes in v7:
time: 118 us
  Pallas kernels  116 us (98%)
  between operations  1.29 us (1%)
    pallas_call x1, Pallas kernels, shards(): pl.pallas_call(functools.partial(kernel, axes), out_shape=(jax.ShapeDtype...  114 us

profile of v7, /device:TPU:1, one launch (start us, length us, event | category | flops | bytes accessed | tf_op | source)
XLA Modules:
  0.0 117.7 jit_solution(1373803748526909467)
XLA Ops:
  1.3 114.4 %shard_map.85 = (bf16[256,384]{1,0:T(8,128)(2,1)}, f32[96,768]{1,0:T(8,128)}, f32[96,768]{1,0:T(8,128)}) custom-call(bf16[256,384]{1,0:T(8,128)(2,1)} %tok_ref.1, bf16[192,768]{1,0:T(8,128)(2,1)} %bitcast.10, bf16[4,48,768]{2,1,0:T(8,128)(2,1)} %bitcast.11, f32[50,72,128]{2,1,0:T(8,128)} %bitcast.9, s32[1]{0:T(128)S(6)} %copy.9.step_in, s32[16]{0:T(128)} %counts_in.1), custom_call_target="tpu_custom_call" | custom-call | tf_op jit(solution)/shard_map/pallas_call | solution.py:786
  115.7 2.0 %shard_map.86 = (bf16[256,384]{1,0:T(8,128)(2,1)}, f32[96,768]{1,0:T(8,128)}, f32[96,768]{1,0:T(8,128)}) custom-call(bf16[256,384]{1,0:T(8,128)(2,1)} %get-tuple-element.9.out_in, f32[96,768]{1,0:T(8,128)} %get-tuple-element.10.up_in, f32[96,768]{1,0:T(8,128)} %get-tuple-element.11.down_in), custom_call_target="tpu_custom_call" | custom-call | tf_op jit(solution)/shard_map/pallas_call | solution.py:805

commit v8 on v7

--- a/solution.py
+++ b/solution.py
@@ -14,16 +14,17 @@
 RA = (32, 32, 32, 16)
 RU = 112
 ORDER = (
-    ("g2", 3), ("g1", 3), ("hc", 0), ("ho", 0), ("g1", 0), ("g4", 3), ("g2", 0), ("g3", 3), ("g1", 1), ("g2", 1),
-    ("g2", 2), ("g1", 2), ("g3", 0), ("g4", 0), ("g5", 3), ("m", 3), ("g3", 1), ("g4", 1), ("g4", 2), ("s0", 3),
-    ("g3", 2), ("g5", 0), ("m", 0), ("g5", 1), ("m", 1), ("s1", 3), ("g5", 2), ("m", 2), ("s0", 0), ("s0", 1),
-    ("s0", 2), ("s2", 3), ("s1", 0), ("s1", 1), ("s1", 2), ("s3", 3), ("s2", 0), ("s2", 1), ("s2", 2), ("s4", 3),
-    ("s3", 0), ("s3", 1), ("s3", 2), ("s4", 0), ("s5", 3), ("s4", 1), ("s4", 2), ("s6", 3), ("s5", 0), ("s5", 1),
-    ("s5", 2), ("s7", 3), ("s6", 0), ("s6", 1), ("s6", 2), ("s8", 3), ("s7", 0), ("s7", 1), ("s7", 2), ("s9", 3),
-    ("s8", 0), ("s10", 3), ("s8", 1), ("s8", 2), ("s9", 0), ("s9", 1), ("s10", 0), ("s9", 2), ("s10", 1), ("s10", 2),
-    ("b", 1), ("b", 0), ("b", 3), ("b", 2), ("r1", 1), ("r2", 1), ("r1", 0), ("r1", 3), ("r1", 2), ("r2", 0),
-    ("r4", 1), ("r3", 1), ("r4", 0), ("r2", 3), ("r4", 3), ("r2", 2), ("r4", 2), ("r3", 0), ("r5", 1), ("r3", 3),
-    ("r3", 2), ("r6", 1), ("r5", 0), ("r6", 0), ("r5", 3), ("r5", 2), ("r6", 3), ("r7", 1), ("r6", 2), ("r7", 0),
+    ("g0", 0), ("g2", 3), ("g1", 3), ("g0", 2), ("hc", 0), ("g1", 1), ("ho", 0), ("g4", 3), ("g2", 1), ("g3", 3),
+    ("g1", 0), ("g3", 1), ("g4", 1), ("g2", 0), ("g1", 2), ("g2", 2), ("g5", 3), ("m", 3), ("g4", 0), ("g3", 0),
+    ("g5", 1), ("m", 1), ("g4", 2), ("g3", 2), ("s0", 3), ("g5", 0), ("s0", 1), ("m", 0), ("g5", 2), ("s1", 3),
+    ("m", 2), ("s0", 0), ("s1", 1), ("s0", 2), ("sl", 1), ("s2", 3), ("s1", 0), ("s2", 1), ("s1", 2), ("tr", 1),
+    ("s3", 3), ("tr", 3), ("s2", 0), ("s3", 1), ("tr", 0), ("tr", 2), ("s2", 2), ("s4", 3), ("s3", 0), ("s4", 1),
+    ("s3", 2), ("s4", 0), ("s5", 3), ("s4", 2), ("s5", 1), ("s6", 3), ("s5", 0), ("s6", 1), ("s5", 2), ("s7", 3),
+    ("s6", 0), ("s6", 2), ("s7", 1), ("s7", 0), ("s7", 2), ("s8", 3), ("s8", 1), ("s8", 0), ("s8", 2), ("s9", 3),
+    ("sl", 0), ("s9", 1), ("s9", 0), ("s10", 3), ("s9", 2), ("s10", 1), ("s10", 0), ("s10", 2), ("b", 1), ("b", 0),
+    ("b", 2), ("b", 3), ("r1", 1), ("r2", 1), ("r1", 0), ("r2", 0), ("r4", 1), ("r1", 2), ("r3", 1), ("r2", 2),
+    ("r3", 0), ("r4", 0), ("r1", 3), ("r4", 2), ("r2", 3), ("r5", 1), ("r5", 0), ("r4", 3), ("r6", 1), ("r3", 2),
+    ("r3", 3), ("r6", 0), ("r5", 2), ("r5", 3), ("r6", 2), ("r7", 1), ("r6", 3), ("r7", 0),
 )
 NZ = 8
 SEQ = 256
@@ -60,8 +61,8 @@
 def kernel(
     axes,
     tok_ref, up_ref, downt_ref, table_ref, step_in, counts_in,
-    out_ref, ug_ref, dg_ref,
-    T, ST, MEAN, RSTD, U, D, N, NTR, HP, SL, ACT, ACTG, PO, PS, PR, ZS, ZR, TAB, step_ref, counts_ref, mod_ref, MODO, GATE, GATEG, TOKT, OTA, OTB, GT, GA, GP,
+    out_to, ug_ref, dg_ref,
+    out_ref, T, ST, MEAN, RSTD, U, D, N, NTR, HP, SL, ACT, ACTG, PO, PS, PR, ZS, ZR, TAB, step_ref, counts_ref, mod_ref, MODO, GATE, GATEG, TOKT, OTA, OTB, GT, GA, GP,
     QV, XBS, XBR, A2S, A2R, A1S, A1R, B2S, B2R, B1S, B1R, AXS, AXR, FS, FO, FR, HS, HR,
     send, recv, local,
 ):
@@ -369,7 +370,6 @@
     tok(3, 1)
     norm(-2, 1)
     norm(2, 1)
-    gd[0].g0()
     for k in (-3, 3):
         for p in range(2):
             norm(k, p)
@@ -377,7 +377,6 @@
     norm(4, 0)
     tok(4, 1)
     norm(4, 1)
-    gd[2].g0()
 
     def hidden(img):
         h = nn(N[img, 0], U[0].reshape(BLK, BLK))
@@ -675,7 +674,8 @@
         red[n].r0()
 
     u_in.wait()
-    begun, mixed_of, swapped, far, put, sloped = [], [], [], [], [], []
+    out_put = pltpu.make_async_copy(out_ref, out_to, local.at[6])
+    begun, mixed_of, swapped, put = [], [], [], []
     gu.g5()
     for what, n in ORDER:
         if what == "hc":
@@ -691,6 +691,10 @@
             if len(mixed_of) == R:
                 send_act(lambda: c)
                 send_act(lambda: oc)
+        elif what == "tr":
+            pl.when(student)(functools.partial(transposed, n))
+        elif what == "sl":
+            pl.when(student)(functools.partial(slopes, n))
         elif what[0] == "s":
             k = int(what[1:])
             if k == 5:
@@ -702,17 +706,13 @@
                 put.append(n)
                 if len(put) == R:
                     out_ref[...] = jnp.transpose(TOKT[...]).astype(BF)
-            if k == 6 and len(sloped) < 2:
-                pl.when(student)(functools.partial(slopes, len(sloped)))
-                sloped.append(n)
-            if k == 8:
-                pl.when(student)(functools.partial(transposed, len(far)))
-                far.append(n)
+                    out_put.start()
         elif what == "b":
             begin(n)
         else:
             getattr(red[n], what)()
 
+    out_put.wait()
     for d in started[None][-N_SEND[None]:]:
         d.wait_send()
 
@@ -729,6 +729,7 @@
     v = pltpu.VMEM
     nred = R
     scratch = [
+        v((SEQ, BLK), BF),
         v((NZ, SEQ, BLK), BF),
         v((NZ, 8, SEQ), F32),
         v((SEQ, 128), F32),
@@ -779,7 +780,7 @@
         v((nred, 2, ROWS, BLK), BF),
         pltpu.SemaphoreType.DMA((sum(N_SEND.values()),)),
         pltpu.SemaphoreType.DMA((N_RECV,)),
-        pltpu.SemaphoreType.DMA((6,)),
+        pltpu.SemaphoreType.DMA((7,)),
     ]
     hbm = pl.BlockSpec(memory_space=pl.ANY)
     vm = pl.BlockSpec(memory_space=pltpu.VMEM)
@@ -791,26 +792,32 @@
             jax.ShapeDtypeStruct((96, 2 * BLK), F32),
         ),
         in_specs=[hbm] * 6,
-        out_specs=(vm, vm, vm),
+        out_specs=(hbm, vm, vm),
         scratch_shapes=scratch,
         compiler_params=pltpu.CompilerParams(
             collective_id=0, has_side_effects=True, vmem_limit_bytes=67043328
         ),
     )(tokens, up_weight[0], downt, table, timesteps, valid_counts)
-    def settle(out_in, up_in, down_in, out_to, up_to, down_to):
-        out_to[...] = out_in[...]
-        up_to[...] = up_in[...]
-        down_to[...] = down_in[...]
-
+    def settle(*refs):
+        came, sems = refs[6:9], refs[9]
+        into = [pltpu.make_async_copy(refs[i], came[i], sems.at[i]) for i in range(3)]
+        outof = [pltpu.make_async_copy(came[i], refs[3 + i], sems.at[3 + i]) for i in range(3)]
+        for d in into:
+            d.start()
+        for d, e in zip(into, outof):
+            d.wait()
+            e.start()
+        for e in outof:
+            e.wait()
+
+    shapes = [((SEQ, BLK), BF), ((96, 2 * BLK), F32), ((96, 2 * BLK), F32)]
     out, up, down = pl.pallas_call(
         settle,
-        out_shape=(
-            jax.ShapeDtypeStruct((SEQ, BLK), BF),
-            jax.ShapeDtypeStruct((96, 2 * BLK), F32),
-            jax.ShapeDtypeStruct((96, 2 * BLK), F32),
-        ),
-        in_specs=[vm] * 3,
-        out_specs=(vm,) * 3,
+        out_shape=tuple(jax.ShapeDtypeStruct(*i) for i in shapes),
+        in_specs=[hbm] * 3,
+        out_specs=(hbm,) * 3,
+        scratch_shapes=[v(*i) for i in shapes] + [pltpu.SemaphoreType.DMA((6,))],
+        compiler_params=pltpu.CompilerParams(vmem_limit_bytes=67043328),
     )(out, up, down)
     return out[None], up, down.T
 

time: 118 us -> 117 us (level)
  no operation moved by 1% of the time
where the time goes in v8:
time: 117 us
  Pallas kernels  116 us (99%)
  between operations  1.45 us (1%)
    pallas_call x1, Pallas kernels, shards(): pl.pallas_call(functools.partial(kernel, axes), out_shape=(jax.ShapeDtype...  114 us

profile of v8, /device:TPU:1, one launch (start us, length us, event | category | flops | bytes accessed | tf_op | source)
XLA Modules:
  0.0 116.9 jit_solution(12916575336402350283)
XLA Ops:
  1.3 113.6 %shard_map.85 = (bf16[256,384]{1,0:T(8,128)(2,1)}, f32[96,768]{1,0:T(8,128)}, f32[96,768]{1,0:T(8,128)}) custom-call(bf16[256,384]{1,0:T(8,128)(2,1)} %tok_ref.1, bf16[192,768]{1,0:T(8,128)(2,1)} %bitcast.10, bf16[4,48,768]{2,1,0:T(8,128)(2,1)} %bitcast.11, f32[50,72,128]{2,1,0:T(8,128)} %bitcast.9, s32[1]{0:T(128)S(6)} %copy.9.step_in, s32[16]{0:T(128)} %counts_in.1), custom_call_target="tpu_custom_call" | custom-call | tf_op jit(solution)/shard_map/pallas_call | solution.py:787
  114.9 1.9 %shard_map.86 = (bf16[256,384]{1,0:T(8,128)(2,1)}, f32[96,768]{1,0:T(8,128)}, f32[96,768]{1,0:T(8,128)}) custom-call(bf16[256,384]{1,0:T(8,128)(2,1)} %get-tuple-element.9.refs_0_, f32[96,768]{1,0:T(8,128)} %get-tuple-element.10.refs_1_, f32[96,768]{1,0:T(8,128)} %get-tuple-element.11.refs_2_), custom_call_target="tpu_custom_call" | custom-call | tf_op jit(solution)/shard_map/pallas_call | solution.py:814

commit v9 on v8

--- a/solution.py
+++ b/solution.py
@@ -14,17 +14,17 @@
 RA = (32, 32, 32, 16)
 RU = 112
 ORDER = (
-    ("g0", 0), ("g2", 3), ("g1", 3), ("g0", 2), ("hc", 0), ("g1", 1), ("ho", 0), ("g4", 3), ("g2", 1), ("g3", 3),
-    ("g1", 0), ("g3", 1), ("g4", 1), ("g2", 0), ("g1", 2), ("g2", 2), ("g5", 3), ("m", 3), ("g4", 0), ("g3", 0),
-    ("g5", 1), ("m", 1), ("g4", 2), ("g3", 2), ("s0", 3), ("g5", 0), ("s0", 1), ("m", 0), ("g5", 2), ("s1", 3),
-    ("m", 2), ("s0", 0), ("s1", 1), ("s0", 2), ("sl", 1), ("s2", 3), ("s1", 0), ("s2", 1), ("s1", 2), ("tr", 1),
-    ("s3", 3), ("tr", 3), ("s2", 0), ("s3", 1), ("tr", 0), ("tr", 2), ("s2", 2), ("s4", 3), ("s3", 0), ("s4", 1),
-    ("s3", 2), ("s4", 0), ("s5", 3), ("s4", 2), ("s5", 1), ("s6", 3), ("s5", 0), ("s6", 1), ("s5", 2), ("s7", 3),
-    ("s6", 0), ("s6", 2), ("s7", 1), ("s7", 0), ("s7", 2), ("s8", 3), ("s8", 1), ("s8", 0), ("s8", 2), ("s9", 3),
-    ("sl", 0), ("s9", 1), ("s9", 0), ("s10", 3), ("s9", 2), ("s10", 1), ("s10", 0), ("s10", 2), ("b", 1), ("b", 0),
-    ("b", 2), ("b", 3), ("r1", 1), ("r2", 1), ("r1", 0), ("r2", 0), ("r4", 1), ("r1", 2), ("r3", 1), ("r2", 2),
-    ("r3", 0), ("r4", 0), ("r1", 3), ("r4", 2), ("r2", 3), ("r5", 1), ("r5", 0), ("r4", 3), ("r6", 1), ("r3", 2),
-    ("r3", 3), ("r6", 0), ("r5", 2), ("r5", 3), ("r6", 2), ("r7", 1), ("r6", 3), ("r7", 0),
+    ("g2", 3), ("g1", 3), ("g0", 2), ("hc", 0), ("ho", 0), ("g1", 0), ("g4", 3), ("g2", 0), ("g3", 3), ("g1", 1),
+    ("g2", 1), ("g2", 2), ("g1", 2), ("g3", 0), ("g4", 0), ("g5", 3), ("m", 3), ("g3", 1), ("g4", 1), ("g4", 2),
+    ("s0", 3), ("g3", 2), ("g5", 0), ("m", 0), ("g5", 1), ("m", 1), ("s1", 3), ("g5", 2), ("m", 2), ("s0", 0),
+    ("s0", 1), ("s0", 2), ("s2", 3), ("s1", 0), ("s1", 1), ("s1", 2), ("s3", 3), ("s2", 0), ("s2", 1), ("s2", 2),
+    ("s4", 3), ("s3", 0), ("s3", 1), ("s3", 2), ("s4", 0), ("s5", 3), ("s4", 1), ("s4", 2), ("s6", 3), ("sl", 0),
+    ("s5", 0), ("s5", 1), ("s5", 2), ("s7", 3), ("s6", 0), ("sl", 1), ("s6", 1), ("s6", 2), ("s8", 3), ("tr", 0),
+    ("s7", 0), ("s7", 1), ("s7", 2), ("s9", 3), ("s8", 0), ("tr", 1), ("s10", 3), ("s8", 1), ("tr", 2), ("s8", 2),
+    ("tr", 3), ("s9", 0), ("s9", 1), ("s10", 0), ("s9", 2), ("s10", 1), ("s10", 2), ("b", 1), ("b", 0), ("b", 2),
+    ("b", 3), ("r1", 1), ("r2", 1), ("r1", 0), ("r2", 0), ("r1", 2), ("r4", 1), ("r2", 2), ("r3", 1), ("r3", 0),
+    ("r4", 0), ("r1", 3), ("r2", 3), ("r4", 2), ("r3", 2), ("r5", 1), ("r5", 0), ("r6", 1), ("r4", 3), ("r3", 3),
+    ("r6", 0), ("r5", 2), ("r6", 2), ("r5", 3), ("r7", 1), ("r6", 3), ("r7", 0),
 )
 NZ = 8
 SEQ = 256
@@ -370,6 +370,7 @@
     tok(3, 1)
     norm(-2, 1)
     norm(2, 1)
+    gd[0].g0()
     for k in (-3, 3):
         for p in range(2):
             norm(k, p)

time: 117 us -> 116 us (level)
  no operation moved by 1% of the time
where the time goes in v9:
time: 116 us
  Pallas kernels  115 us (99%)
  between operations  1.45 us (1%)
    pallas_call x1, Pallas kernels, shards(): pl.pallas_call(functools.partial(kernel, axes), out_shape=(jax.ShapeDtype...  113 us

profile of v9, /device:TPU:1, one launch (start us, length us, event | category | flops | bytes accessed | tf_op | source)
XLA Modules:
  0.0 116.2 jit_solution(10316642931171724583)
XLA Ops:
  1.3 112.8 %shard_map.85 = (bf16[256,384]{1,0:T(8,128)(2,1)}, f32[96,768]{1,0:T(8,128)}, f32[96,768]{1,0:T(8,128)}) custom-call(bf16[256,384]{1,0:T(8,128)(2,1)} %tok_ref.1, bf16[192,768]{1,0:T(8,128)(2,1)} %bitcast.10, bf16[4,48,768]{2,1,0:T(8,128)(2,1)} %bitcast.11, f32[50,72,128]{2,1,0:T(8,128)} %bitcast.9, s32[1]{0:T(128)S(6)} %copy.9.step_in, s32[16]{0:T(128)} %counts_in.1), custom_call_target="tpu_custom_call" | custom-call | tf_op jit(solution)/shard_map/pallas_call | solution.py:788
  114.1 1.9 %shard_map.86 = (bf16[256,384]{1,0:T(8,128)(2,1)}, f32[96,768]{1,0:T(8,128)}, f32[96,768]{1,0:T(8,128)}) custom-call(bf16[256,384]{1,0:T(8,128)(2,1)} %get-tuple-element.9.refs_0_, f32[96,768]{1,0:T(8,128)} %get-tuple-element.10.refs_1_, f32[96,768]{1,0:T(8,128)} %get-tuple-element.11.refs_2_), custom_call_target="tpu_custom_call" | custom-call | tf_op jit(solution)/shard_map/pallas_call | solution.py:815

commit v10 on v9

--- a/solution.py
+++ b/solution.py
@@ -18,10 +18,10 @@
     ("g2", 1), ("g2", 2), ("g1", 2), ("g3", 0), ("g4", 0), ("g5", 3), ("m", 3), ("g3", 1), ("g4", 1), ("g4", 2),
     ("s0", 3), ("g3", 2), ("g5", 0), ("m", 0), ("g5", 1), ("m", 1), ("s1", 3), ("g5", 2), ("m", 2), ("s0", 0),
     ("s0", 1), ("s0", 2), ("s2", 3), ("s1", 0), ("s1", 1), ("s1", 2), ("s3", 3), ("s2", 0), ("s2", 1), ("s2", 2),
-    ("s4", 3), ("s3", 0), ("s3", 1), ("s3", 2), ("s4", 0), ("s5", 3), ("s4", 1), ("s4", 2), ("s6", 3), ("sl", 0),
-    ("s5", 0), ("s5", 1), ("s5", 2), ("s7", 3), ("s6", 0), ("sl", 1), ("s6", 1), ("s6", 2), ("s8", 3), ("tr", 0),
-    ("s7", 0), ("s7", 1), ("s7", 2), ("s9", 3), ("s8", 0), ("tr", 1), ("s10", 3), ("s8", 1), ("tr", 2), ("s8", 2),
-    ("tr", 3), ("s9", 0), ("s9", 1), ("s10", 0), ("s9", 2), ("s10", 1), ("s10", 2), ("b", 1), ("b", 0), ("b", 2),
+    ("s4", 3), ("tr", 0), ("s3", 0), ("s3", 1), ("s3", 2), ("s4", 0), ("tr", 1), ("s5", 3), ("s4", 1), ("tr", 2),
+    ("s4", 2), ("tr", 3), ("s6", 3), ("sl", 0), ("s5", 0), ("s5", 1), ("s5", 2), ("s7", 3), ("s6", 0), ("sl", 1),
+    ("s6", 1), ("s6", 2), ("s8", 3), ("s7", 0), ("s7", 1), ("s7", 2), ("s9", 3), ("s8", 0), ("s10", 3), ("s8", 1),
+    ("s8", 2), ("s9", 0), ("s9", 1), ("s10", 0), ("s9", 2), ("s10", 1), ("s10", 2), ("b", 1), ("b", 0), ("b", 2),
     ("b", 3), ("r1", 1), ("r2", 1), ("r1", 0), ("r2", 0), ("r1", 2), ("r4", 1), ("r2", 2), ("r3", 1), ("r3", 0),
     ("r4", 0), ("r1", 3), ("r2", 3), ("r4", 2), ("r3", 2), ("r5", 1), ("r5", 0), ("r6", 1), ("r4", 3), ("r3", 3),
     ("r6", 0), ("r5", 2), ("r6", 2), ("r5", 3), ("r7", 1), ("r6", 3), ("r7", 0),

time: 116 us -> 117 us (level)
  no operation moved by 1% of the time
where the time goes in v10:
time: 117 us; the launch traced here: 116 us
  Pallas kernels  115 us (98%)
  between operations  1.45 us (1%)
    pallas_call x1, Pallas kernels, shards(): pl.pallas_call(functools.partial(kernel, axes), out_shape=(jax.ShapeDtype...  113 us

profile of v10, /device:TPU:1, one launch (start us, length us, event | category | flops | bytes accessed | tf_op | source)
XLA Modules:
  0.0 116.5 jit_solution(1942064204610966906)
XLA Ops:
  1.3 113.1 %shard_map.85 = (bf16[256,384]{1,0:T(8,128)(2,1)}, f32[96,768]{1,0:T(8,128)}, f32[96,768]{1,0:T(8,128)}) custom-call(bf16[256,384]{1,0:T(8,128)(2,1)} %tok_ref.1, bf16[192,768]{1,0:T(8,128)(2,1)} %bitcast.10, bf16[4,48,768]{2,1,0:T(8,128)(2,1)} %bitcast.11, f32[50,72,128]{2,1,0:T(8,128)} %bitcast.9, s32[1]{0:T(128)S(6)} %copy.9.step_in, s32[16]{0:T(128)} %counts_in.1), custom_call_target="tpu_custom_call" | custom-call | tf_op jit(solution)/shard_map/pallas_call | solution.py:788
  114.4 1.9 %shard_map.86 = (bf16[256,384]{1,0:T(8,128)(2,1)}, f32[96,768]{1,0:T(8,128)}, f32[96,768]{1,0:T(8,128)}) custom-call(bf16[256,384]{1,0:T(8,128)(2,1)} %get-tuple-element.9.refs_0_, f32[96,768]{1,0:T(8,128)} %get-tuple-element.10.refs_1_, f32[96,768]{1,0:T(8,128)} %get-tuple-element.11.refs_2_), custom_call_target="tpu_custom_call" | custom-call | tf_op jit(solution)/shard_map/pallas_call | solution.py:815
